TPU v7x, 256 devices: a whole 4x4x8 slice. The times are simulated.
256 devices in a mesh: rows: 64 (over x, z, core), cols: 4 (over y).
Axes of the slice: x: 4, y: 4, z: 8, core: 2. Of those that a mesh axis runs over, the one named last changes fastest.
Arguments:
- column_lists: int32 [256, 13], replicated, may hold values from -1 to 255, as said below
- block_values: bfloat16 [256, 13, 128, 128], P('rows'), as said below
Outputs:
- purified: bfloat16 [256, 13, 128, 128], P('rows', None, None, 'cols')
Inputs may be any that keep to these rules, and one draw needn't show every extreme that they name: `column_lists`: slot (13 - 1) // 2 of row i holds i. Slot s of row i holds -1 or a row j, and then slot 12 - s of row j holds i. There is an ordering of the rows, taken cyclically, in which the row in slot s of row i stands s - (13 - 1) // 2 places after row i. With owners the aligned groups of 4 rows, the slots of one owner's rows hold at most 2 rows of any one other owner, and some pair of owners has exactly 2. Over the slots s of one owner's rows that hold rows of one other owner, the sum of 13 - |s - (13 - 1) // 2| is at most 16, and exactly 16 for some pair of owners. block_values[j, 12 - s] is the transpose of block_values[i, s] where slot s of row i holds j; blocks of empty slots are zero.
All inputs are finite; a program needn't handle non-finite values.
Results may differ from a plain program's by a relative error of at most 0.0039.
Values may be sent and summed in bfloat16 or wider, within the bound.
No kernel may reach another device: no remote copies, remote signals or barrier semaphores. Data moves between devices by JAX's collectives and lax.ppermute only.
A program may use at most 128 MiB of HBM per device.

v0:
```python
import jax
import jax.numpy as jnp
from jax import lax
from jax.sharding import PartitionSpec as P

CAP = 2


def body(column_lists, block_values):
    rows_here = block_values.shape[0]
    slot_count = block_values.shape[1]
    block_size = block_values.shape[2]
    middle = (slot_count - 1) // 2
    owners = lax.axis_size("rows")
    strip_width = block_size // lax.axis_size("cols")
    row_index = lax.axis_index("rows")
    column_part = lax.axis_index("cols")
    all_rows = column_lists.shape[0]
    present = column_lists >= 0
    target = jnp.maximum(column_lists, 0)
    owner_of = target // rows_here
    home_owner = (jnp.arange(all_rows, dtype=jnp.int32) // rows_here)[:, None]
    crossing = present & (owner_of != home_owner)
    dest_hot = (
        crossing[:, :, None] & (owner_of[:, :, None] == jnp.arange(owners, dtype=jnp.int32))
    ).astype(jnp.int32)
    first_row = row_index * rows_here
    own_present = lax.dynamic_slice_in_dim(present, first_row, rows_here, 0)
    my_cross = lax.dynamic_slice_in_dim(crossing, first_row, rows_here, 0)
    my_owner = lax.dynamic_slice_in_dim(owner_of, first_row, rows_here, 0)
    my_target = lax.dynamic_slice_in_dim(target, first_row, rows_here, 0)
    full_rows = jnp.where(
        own_present[:, :, None, None], block_values, jnp.zeros((), block_values.dtype)
    )
    own_strip = lax.dynamic_slice_in_dim(full_rows, column_part * strip_width, strip_width, 3)
    slot_ids = jnp.arange(slot_count, dtype=jnp.int32)
    running = jnp.cumsum(dest_hot.reshape(owners, rows_here * slot_count, owners), axis=1)
    running = running.reshape(all_rows, slot_count, owners)
    ranking = jnp.sum(running * dest_hot, axis=2) - 1
    my_rank = lax.dynamic_slice_in_dim(ranking, first_row, rows_here, 0)
    filler = jnp.zeros((1, slot_count - 1, block_size, strip_width), own_strip.dtype)
    local_stack = jnp.concatenate([own_strip[:, : slot_count - 1], own_strip[:, 1:], filler], 0)
    zero_entry = 2 * rows_here
    slot_of = jnp.where(my_cross, my_owner * CAP + my_rank, owners * CAP)
    stack_entry = (
        jnp.arange(rows_here, dtype=jnp.int32)[:, None]
        + jnp.where(slot_ids < middle, 0, rows_here)[None, :]
    )
    source = jnp.full((owners * CAP + 1,), zero_entry, jnp.int32)
    source = source.at[slot_of.reshape(-1)].set(stack_entry.reshape(-1))[: owners * CAP]
    outgoing = local_stack[source]
    back_rank = ranking[my_target, (slot_count - 1 - slot_ids)[None, :]]
    local_pick = (
        owners * CAP + my_target - first_row + jnp.where(slot_ids > middle, 0, rows_here)[None, :]
    )
    remote_pick = my_owner * CAP + back_rank
    empty_entry = owners * CAP + zero_entry
    table_pick = jnp.where(
        own_present & (my_owner == row_index),
        local_pick,
        jnp.where(own_present, remote_pick, empty_entry),
    )
    table_pick = table_pick.at[:, middle].set(empty_entry)
    arrived = lax.all_to_all(outgoing, "rows", split_axis=0, concat_axis=0, tiled=True)
    lookup = jnp.concatenate([arrived, local_stack], 0)
    picked = lookup[table_pick]
    by_slot = []
    for slot_index in range(slot_count):
        offset = slot_index - middle
        if offset == 0:
            by_slot.append(own_strip)
        elif offset > 0:
            by_slot.append(
                jnp.pad(
                    picked[:, slot_index, : slot_count - offset],
                    ((0, 0), (offset, 0), (0, 0), (0, 0)),
                )
            )
        else:
            by_slot.append(
                jnp.pad(
                    picked[:, slot_index, -offset - 1 :], ((0, 0), (0, -offset), (0, 0), (0, 0))
                )
            )
    windows = jnp.stack(by_slot, 1)
    square_sum = jnp.einsum(
        "iapq,iasqc->ispc", full_rows, windows, preferred_element_type=jnp.float32
    )
    square = jnp.where(own_present[:, :, None, None], square_sum, 0.0).astype(jnp.bfloat16)
    cube_sum = jnp.einsum(
        "iapq,iasqc->ispc",
        lax.all_gather(square, "cols", axis=3, tiled=True),
        windows,
        preferred_element_type=jnp.float32,
    )
    purified = jnp.where(
        own_present[:, :, None, None], 3.0 * square.astype(jnp.float32) - 2.0 * cube_sum, 0.0
    )
    return purified.astype(jnp.bfloat16)


def solution(mesh):
    in_specs = (P(), P("rows", None, None, None))
    out_specs = P("rows", None, None, "cols")
    return jax.shard_map(body, mesh=mesh, in_specs=in_specs, out_specs=out_specs, check_vma=False)
```

profile of v0, /device:TPU:8, one launch (start us, length us, event | category | flops | bytes accessed | tf_op | source)
XLA Modules:
  0.0 388.3 jit_solution(5772552660954711740)
XLA Ops:
  6.6 0.8 copy.54
  8.1 2.7 select_reduce_fusion
  11.0 1.0 gather_fusion.1
  12.1 2.8 copy.55
  15.1 0.7 scatter_custom_fusion
  16.2 1.1 copy-done
  17.6 8.0 %gather_fusion = bf16[128,12,128,32]{2,3,1,0:T(8,128)(2,1)} fusion(bf16[9,12,128,32]{2,3,1,0:T(8,128)(2,1)S(1)} %pad_maximum_fusion.1, s32[1024]{0:T(1024)S(1)} %pad_clamp_fusion.1), kind=kCustom, calls=%fused_computation | custom fusion | bytes 25166336 | tf_op jit(solution)/shard_map/gather | solution.py:51
  25.7 12.2 %all-to-all-start = ((bf16[128,12,128,32]{2,3,1,0:T(8,128)(2,1)}), bf16[128,12,128,32]{2,3,1,0:T(8,128)(2,1)}, u32[]{:S(2)}, u32[]{:S(2)}) async-start(bf16[128,12,128,32]{2,3,1,0:T(8,128)(2,1)} %gather_fusion), calls=%async_computation | async-start | bytes 25165824 | tf_op jit(solution)/shard_map/all_to_all | solution.py:64
  37.9 0.7 compare_reduce_fusion
  38.6 0.8 slice_select_fusion
  39.7 272.9 %all-to-all-done = bf16[128,12,128,32]{2,3,1,0:T(8,128)(2,1)} async-done(((bf16[128,12,128,32]{2,3,1,0:T(8,128)(2,1)}), bf16[128,12,128,32]{2,3,1,0:T(8,128)(2,1)}, u32[]{:S(2)}, u32[]{:S(2)}) %all-to-all-start) | async-done | bytes 12582944 | tf_op jit(solution)/shard_map/all_to_all | solution.py:64
  312.7 14.4 %pad_maximum_fusion = bf16[137,12,128,32]{2,3,1,0:T(8,128)(2,1)} fusion(bf16[1,12,128,32]{2,3,1,0:T(8,128)(2,1)S(1)} %broadcast_in_dim.85, bf16[4,12,128,32]{2,3,1,0:T(8,128)(2,1)S(1)} %copy-done.4, bf16[4,12,128,32]{2,3,1,0:T(8,128)(2,1)S(1)} %copy-done.2, bf16[128,12,128,32]{2,3,1,0:T(8,128)(2,1)} %all-to-all-done), kind=kLoop, calls=%fused_computation.4 | loop fusion | flops 20201472 | bytes 26935296 | tf_op jit(solution)/shard_map/concatenate | solution.py:65
  327.1 8.4 %gather_fusion.2 = bf16[52,12,128,32]{2,3,1,0:T(8,128)(2,1)} fusion(bf16[137,12,128,32]{2,3,1,0:T(8,128)(2,1)} %pad_maximum_fusion, s32[1024]{0:T(1024)S(1)} %pad_clamp_fusion), kind=kCustom, calls=%fused_computation.2 | custom fusion | bytes 10223824 | tf_op jit(solution)/shard_map/gather | solution.py:66
  335.4 1.1 slice_bitcast_fusion.10
  336.5 1.1 slice_bitcast_fusion.8
  337.6 1.1 slice_bitcast_fusion.6
  338.7 1.1 slice_bitcast_fusion.4
  339.8 1.1 slice_bitcast_fusion.2
  341.0 1.2 slice_bitcast_fusion
  342.6 1.1 bitcast_dynamic-update-slice_fusion.6
  344.1 2.4 copy-done.5
  346.6 2.4 fusion.35
  349.0 27.0 %all-gather.2.cloned.1.call-done = bf16[4,13,128,128]{2,3,1,0:T(8,128)(2,1)} async-done(((bf16[4,13,128,32]{2,3,1,0:T(8,128)(2,1)}), bf16[4,13,128,128]{2,3,1,0:T(8,128)(2,1)}) %all-gather.2.cloned.1.call-update) | async-done | bytes 1703952 | tf_op jit(solution)/shard_map/all_gather | solution.py:92
  376.0 5.4 %fusion.26 = bf16[4,13,128,32]{2,3,1,0:T(8,128)(2,1)} fusion(bf16[4,13,13,128,32]{3,4,1,2,0:T(8,128)(2,1)} %copy-done.5, bf16[4,13,128,128]{2,3,1,0:T(8,128)(2,1)} %all-gather.2.cloned.1.call-done, bf16[4,13,128,32]{2,3,1,0:T(8,128)(2,1)} %fusion.35, pred[4,13]{1,0:T(4,128)(4,1)S(1)} %get-tuple-element.18), kind=kOutput, calls=%fused_computation.21 | convolution fusion | flops 710115328 | bytes 8093748 | tf_op jit(solution)/shard_map/iapq,iasqc->ispc/dot_general | solution.py:90
  (54 shorter events, 3.0 us)
Async XLA Ops:
  16.1 1.2 copy-start
  16.2 1.2 copy-start.1
  16.2 1.3 copy-start.3
  25.7 287.0 %copy-start.2 = (bf16[4,12,128,32]{2,3,1,0:T(8,128)(2,1)S(1)}, bf16[4,12,128,32]{2,3,1,0:T(8,128)(2,1)}, u32[]{:S(2)}) copy-start(bf16[4,12,128,32]{2,3,1,0:T(8,128)(2,1)} %copy-done.1) | copy-start | bytes 1179652
  25.7 287.0 %copy-start.4 = (bf16[4,12,128,32]{2,3,1,0:T(8,128)(2,1)S(1)}, bf16[4,12,128,32]{2,3,1,0:T(8,128)(2,1)}, u32[]{:S(2)}) copy-start(bf16[4,12,128,32]{2,3,1,0:T(8,128)(2,1)} %copy-done.3) | copy-start | bytes 1179652
  25.7 287.0 %all-to-all-start = ((bf16[128,12,128,32]{2,3,1,0:T(8,128)(2,1)}), bf16[128,12,128,32]{2,3,1,0:T(8,128)(2,1)}, u32[]{:S(2)}, u32[]{:S(2)}) async-start(bf16[128,12,128,32]{2,3,1,0:T(8,128)(2,1)} %gather_fusion), calls=%async_computation | async-start | bytes 25165824 | tf_op jit(solution)/shard_map/all_to_all | solution.py:64
  37.9 338.1 %all-gather.2.cloned.1.call-start = ((), (), s32[]{:S(2)}) async-start(), calls=%async_computation.1 | async-start | bytes 2129920 | tf_op jit(solution)/shard_map/all_gather | solution.py:92
  344.1 2.4 copy-start.5
Sparse Core Ops, SparseCore 0:
  349.1 26.8 all-gather.1
where the time goes:
time: 391 us; the launch traced here: 388 us
  waiting for transfers between devices  300 us (77%)
  local copies, waits for them, and re-layouts  35.4 us (9%)
  other arithmetic  19.1 us (5%)
  between operations  13.7 us (4%)
  starting transfers between devices  12.3 us (3%)
  matrix products  7.86 us (2%)
    all_to_all x1, waiting for transfers between devices, body(): lax.all_to_all(outgoing, 'rows', split_axis=0, concat_axis=0, tiled=True)  273 us
    all_gather x1, waiting for transfers between devices, body(): lax.all_gather(square, 'cols', axis=3, tiled=True)  27 us
    concatenate x1, other arithmetic, body(): lookup = jnp.concatenate([arrived, local_stack], 0)  14.4 us
    all_to_all x1, starting transfers between devices, body(): lax.all_to_all(outgoing, 'rows', split_axis=0, concat_axis=0, tiled=True)  12.2 us
    unnamed x26, local copies, waits for them, and re-layouts  9.2 us
    gather x1, local copies, waits for them, and re-layouts, body(): picked = lookup[table_pick]  8.37 us
    gather x1, local copies, waits for them, and re-layouts, body(): outgoing = local_stack[source]  8.05 us
  transfers between devices with their start and end apart: 2, of which 2 were waited for; matrix products, arithmetic and copies ran while one was open for 0% of the time, Pallas kernels for 0%

commit v1 on v0

v1 whole, which is shorter than its diff:
```python
import functools

import jax
import jax.numpy as jnp
import numpy as np
from jax import lax
from jax.experimental import pallas as pl
from jax.experimental.pallas import tpu as pltpu
from jax.sharding import Mesh
from jax.sharding import PartitionSpec as P

X, Z, CORE, Y = 4, 8, 2, 4
BLK = 128
SLOTS = 13
MID = 6
HALF = 7
ROWS_HERE = 4
PIECES = X * Y
TILE = BLK // PIECES
AXES = ("x", "z", "core", "y")


def wanted():
    pairs = []
    for a in range(SLOTS):
        if a == MID:
            continue
        for s in range(a, min(SLOTS, a + HALF)):
            if s != MID:
                pairs.append((a, s))
    return pairs


WANTED = wanted()
COUNT = len(WANTED)


def runs():
    out = []
    for place, (a, s) in enumerate(WANTED):
        d = s - a
        if out and out[-1][0] == a and out[-1][1] + out[-1][2] == d:
            out[-1][2] += 1
        else:
            out.append([a, d, 1, place])
    return [tuple(r) for r in out]


RUNS = runs()


def select_kernel(lists, where, *refs):
    pieces = refs[: 2 * Z]
    out, held, sems = refs[2 * Z :]
    z, core = where[1], where[2]
    copies = []
    for n in range(2 * Z):
        step, other = n % Z, n // Z
        place = lax.rem(z + step, Z) + Z * lax.rem(core + other, 2)
        copies.append(pltpu.make_async_copy(pieces[n], held.at[place], sems.at[n]))
    for copy in copies:
        copy.start()
    for copy in copies:
        copy.wait()

    def one(t, carry):
        owner = ((t // Y) * Z + z) * CORE + core
        row = ROWS_HERE * owner + lax.rem(t, Y)
        for a, d, length, first in RUNS:
            k = jnp.maximum(lists[row * SLOTS + a], 0)
            r = k // ROWS_HERE
            place = lax.rem(r, 2) * Z + lax.rem(r // 2, Z)
            inner = (r // (2 * Z)) * ROWS_HERE + lax.rem(k, ROWS_HERE)
            out[t, first : first + length] = held[place, inner, d : d + length]
        return carry

    lax.fori_loop(0, PIECES, one, 0)


def select(lists, where, pieces):
    smem = pl.BlockSpec(memory_space=pltpu.SMEM)
    hbm = pl.BlockSpec(memory_space=pl.ANY)
    return pl.pallas_call(
        select_kernel,
        out_shape=jax.ShapeDtypeStruct((PIECES, COUNT, TILE, BLK), jnp.bfloat16),
        in_specs=[smem, smem] + [hbm] * (2 * Z),
        out_specs=pl.BlockSpec(memory_space=pltpu.VMEM),
        scratch_shapes=[
            pltpu.VMEM((2 * Z, X * ROWS_HERE, HALF, TILE, BLK), jnp.bfloat16),
            pltpu.SemaphoreType.DMA((2 * Z,)),
        ],
        name="select",
    )(lists, where, *pieces)


def groups():
    out = []
    for s in range(0, SLOTS, 2):
        n = min(2, SLOTS - s)
        low = max(0, s - MID)
        high = min(SLOTS - 1, s + n - 1 + MID)
        out.append((s, n, low, high - low + 1))
    return out


GROUPS = groups()


def purify_kernel(lists, where, got, own, out, u, w, sq, sems):
    row = ROWS_HERE * ((where[0] * Z + where[1]) * CORE + where[2]) + where[3]
    copies = [pltpu.make_async_copy(got.at[p], u.at[:, p], sems.at[p]) for p in range(PIECES)]
    for s in range(SLOTS):
        copies.append(
            pltpu.make_async_copy(
                own.at[where[3], s],
                w.at[MID * BLK : (MID + 1) * BLK, s * BLK : (s + 1) * BLK],
                sems.at[PIECES + s],
            )
        )
    for copy in copies:
        copy.start()

    def blk(a):
        return slice(a * BLK, (a + 1) * BLK)

    for a in range(SLOTS - HALF):
        w[blk(a), blk(a + HALF)] = jnp.zeros((BLK, BLK), jnp.bfloat16)
        w[blk(a + HALF), blk(a)] = jnp.zeros((BLK, BLK), jnp.bfloat16)
    for copy in copies:
        copy.wait()
    for s in range(SLOTS):
        if s != MID:
            w[blk(s), blk(MID)] = w[blk(MID), blk(s)].T
    for place, (a, s) in enumerate(WANTED):
        value = u[place].reshape(BLK, BLK)
        w[blk(a), blk(s)] = value
        if a != s:
            w[blk(s), blk(a)] = value.T

    def mask(value, s):
        return jnp.where(lists[row * SLOTS + s] >= 0, value, jnp.zeros_like(value))

    def span(first, n):
        return slice(first * BLK, (first + n) * BLK)

    for s, n, low, count in GROUPS:
        total = jnp.dot(
            w[blk(MID), span(low, count)], w[span(low, count), span(s, n)], preferred_element_type=jnp.float32
        )
        for j in range(n):
            sq[:, blk(s + j)] = mask(total[:, blk(j)], s + j).astype(jnp.bfloat16)
    for s, n, low, count in GROUPS:
        total = jnp.dot(sq[:, span(low, count)], w[span(low, count), span(s, n)], preferred_element_type=jnp.float32)
        for j in range(n):
            value = 3.0 * sq[:, blk(s + j)].astype(jnp.float32) - 2.0 * total[:, blk(j)]
            value = mask(value, s + j).T.astype(jnp.bfloat16)
            for part in range(Y):
                out[part, s + j] = value[part * 32 : (part + 1) * 32]


def purify(lists, where, got, own):
    smem = pl.BlockSpec(memory_space=pltpu.SMEM)
    hbm = pl.BlockSpec(memory_space=pl.ANY)
    return pl.pallas_call(
        purify_kernel,
        out_shape=jax.ShapeDtypeStruct((Y, SLOTS, BLK // Y, BLK), jnp.bfloat16),
        in_specs=[smem, smem, hbm, hbm],
        out_specs=pl.BlockSpec(memory_space=pltpu.VMEM),
        scratch_shapes=[
            pltpu.VMEM((COUNT, PIECES, TILE, BLK), jnp.bfloat16),
            pltpu.VMEM((SLOTS * BLK, SLOTS * BLK), jnp.bfloat16),
            pltpu.VMEM((BLK, SLOTS * BLK), jnp.bfloat16),
            pltpu.SemaphoreType.DMA((PIECES + SLOTS,)),
        ],
        name="purify",
    )(lists, where, got, own)


def shift(value, axis, size, step):
    return lax.ppermute(value, axis, [((i + step) % size, i) for i in range(size)])


def gather_z(own):
    up, down = [own], [own]
    for _ in range(3):
        up.append(shift(up[-1], "z", Z, 1))
        down.append(shift(down[-1], "z", Z, -1))
    half = own.shape[0] // 2
    far = jnp.concatenate([shift(up[3][:half], "z", Z, 1), shift(down[3][half:], "z", Z, -1)], 0)
    return [own, up[1], up[2], up[3], far, down[3], down[2], down[1]]


def body(column_lists, block_values):
    lists = column_lists.reshape(-1)
    where = jnp.stack([lax.axis_index(a) for a in AXES]).astype(jnp.int32)
    tiles = block_values[:, MID:].reshape(ROWS_HERE, HALF, X, Y, TILE, BLK)
    mine = lax.dynamic_index_in_dim(tiles, where[3], 3, keepdims=False)
    mine = mine.transpose(2, 0, 1, 3, 4)
    part = lax.all_to_all(mine, "x", 0, 0, tiled=True)
    part = part.reshape(X * ROWS_HERE, HALF, TILE, BLK)
    here = gather_z(part)
    there = [shift(p, "core", CORE, 1) for p in here]
    asked = select(lists, where, here + there)
    got = lax.all_to_all(asked, ("x", "y"), 0, 0, tiled=True)
    strips = purify(lists, where, got, block_values)
    mixed = lax.all_to_all(strips, "y", 0, 0, tiled=True)
    return mixed.transpose(0, 1, 3, 2)


def solution(mesh):
    fine = Mesh(mesh.devices.reshape(X, Z, CORE, Y), AXES)
    rows = ("x", "z", "core")
    return jax.shard_map(
        body, mesh=fine, in_specs=(P(), P(rows)), out_specs=P(rows, None, None, "y"), check_vma=False
    )
```

time: 391 us -> 109 us (0.28)
  waiting for transfers between devices: 300 us -> 19.4 us
  blocking collectives: 0 us -> 51.9 us
  local copies, waits for them, and re-layouts: 35.4 us -> 3.69 us
  other arithmetic: 19.1 us -> 0.66 us
  Pallas kernels: 0 us -> 13.7 us
  between operations: 13.7 us -> 0.22 us
  matrix products: 7.86 us -> 0 us
  starting transfers between devices: 12.3 us -> 19.2 us
    all_to_all x1 -> x0, waiting for transfers between devices: 273 us -> none  [body(): lax.all_to_all(outgoing, 'rows', split_axis=0, concat_axis=0, tiled=True)]
    all_to_all x0 -> x3, blocking collectives: none -> 51.9 us  [the longest x1 30.1 us: body(): got = lax.all_to_all(asked, ('x', 'y'), 0, 0, tiled=True)]
    all_gather x1 -> x0, waiting for transfers between devices: 27 us -> none  [body(): lax.all_gather(square, 'cols', axis=3, tiled=True)]
    ppermute x0 -> x16, waiting for transfers between devices: none -> 19.4 us  [shift(): lax.ppermute(value, axis, [((i + step) % size, i) for i in range(size)])]
    ppermute x0 -> x16, starting transfers between devices: none -> 19.2 us  [shift(): lax.ppermute(value, axis, [((i + step) % size, i) for i in range(size)])]
    gather x4 -> x0, local copies, waits for them, and re-layouts: 17.5 us -> none  [the longest x1 8.37 us: body(): picked = lookup[table_pick]]
    concatenate x4 -> x0, other arithmetic: 14.5 us -> none  [the longest x1 14.4 us: body(): lookup = jnp.concatenate([arrived, local_stack], 0)]
    pallas_call x0 -> x2, Pallas kernels: none -> 13.7 us  [the longest x1 8.37 us: select(): pl.pallas_call(select_kernel, out_shape=jax.ShapeDtypeStruct((PIECES, COU...]
  transfers between devices with their start and end apart: 2 -> 16, of which waited for: 2 -> 6; matrix products, arithmetic and copies ran while one was open for 0% -> 1% of each run, Pallas kernels for 0% -> 0%
where the time goes in v1:
time: 109 us
  blocking collectives  51.9 us (48%)
  waiting for transfers between devices  19.4 us (18%)
  starting transfers between devices  19.2 us (18%)
  Pallas kernels  13.7 us (13%)
  local copies, waits for them, and re-layouts  3.69 us (3%)
    all_to_all x1, blocking collectives, body(): got = lax.all_to_all(asked, ('x', 'y'), 0, 0, tiled=True)  30.1 us
    ppermute x16, waiting for transfers between devices, shift(): lax.ppermute(value, axis, [((i + step) % size, i) for i in range(size)])  19.4 us
    ppermute x16, starting transfers between devices, shift(): lax.ppermute(value, axis, [((i + step) % size, i) for i in range(size)])  19.2 us
    all_to_all x1, blocking collectives, body(): mixed = lax.all_to_all(strips, 'y', 0, 0, tiled=True)  11.3 us
    all_to_all x1, blocking collectives, body(): part = lax.all_to_all(mine, 'x', 0, 0, tiled=True)  10.6 us
    pallas_call x1, Pallas kernels, select(): pl.pallas_call(select_kernel, out_shape=jax.ShapeDtypeStruct((PIECES, COU...  8.37 us
    pallas_call x1, Pallas kernels, purify(): pl.pallas_call(purify_kernel, out_shape=jax.ShapeDtypeStruct((Y, SLOTS, B...  5.31 us
  transfers between devices with their start and end apart: 16, of which 6 were waited for; matrix products, arithmetic and copies ran while one was open for 1% of the time, Pallas kernels for 0%

profile of v1, /device:TPU:8, one launch (start us, length us, event | category | flops | bytes accessed | tf_op | source)
XLA Modules:
  0.0 108.7 jit_solution(12968294818353445706)
XLA Ops:
  0.0 1.2 %slice-done = bf16[4,7,128,128]{3,2,1,0:T(8,128)(2,1)S(1)} async-done(((bf16[4,13,128,128]{3,2,1,0:T(8,128)(2,1)}), bf16[4,7,128,128]{3,2,1,0:T(8,128)(2,1)S(1)}, s32[]{:S(2)}) %slice-start) | async-done | bytes 917528 | tf_op jit(solution)/shard_map/slice | solution.py:196
  1.2 10.6 %all_to_all.15 = bf16[4,4,7,8,128]{4,3,2,1,0:T(8,128)(2,1)S(1)} all-to-all(bf16[4,4,7,8,128]{4,3,2,1,0:T(8,128)(2,1)S(1)} %copy_bitcast_fusion), channel_id=1, replica_groups=mesh['x'=4,'z'=8,'core'=2,'y'=4] {'x'}, dimensions={0} | all-to-all | bytes 458752 | tf_op jit(solution)/shard_map/all_to_all | solution.py:199
  11.8 5.9 %collective-permute-start = (bf16[16,7,8,128]{3,2,1,0:T(8,128)(2,1)S(1)}, bf16[16,7,8,128]{3,2,1,0:T(8,128)(2,1)S(1)}, u32[]{:S(2)}, u32[]{:S(2)}) collective-permute-start(bf16[16,7,8,128]{3,2,1,0:T(8,128)(2,1)S(1)} %bitcast.13), channel_id=1, source_target_pairs={{8,0},{16,8},{24,16},{32,24},{40,32},{48,40},{56,48},{0,56},{9,1},... | collective-permute-start | bytes 688136 | tf_op jit(solution)/shard_map/ppermute | solution.py:180
  17.7 3.5 %collective-permute-done.refs_1_ = bf16[16,7,8,128]{3,2,1,0:T(8,128)(2,1)S(1)} collective-permute-done((bf16[16,7,8,128]{3,2,1,0:T(8,128)(2,1)S(1)}, bf16[16,7,8,128]{3,2,1,0:T(8,128)(2,1)S(1)}, u32[]{:S(2)}, u32[]{:S(2)}) %collective-permute-start) | collective-permute-done | bytes 229408 | tf_op jit(solution)/shard_map/ppermute | solution.py:180
  21.2 3.7 %collective-permute-start.1 = (bf16[16,7,8,128]{3,2,1,0:T(8,128)(2,1)S(1)}, bf16[16,7,8,128]{3,2,1,0:T(8,128)(2,1)S(1)}, u32[]{:S(2)}, u32[]{:S(2)}) collective-permute-start(bf16[16,7,8,128]{3,2,1,0:T(8,128)(2,1)S(1)} %collective-permute-done.refs_1_), channel_id=1, source_target_pairs={{8,0},{16,8},{24,16},{32,24},{40,32},{48,40},{56,48},{0,56},{9,1},... | collective-permute-start | bytes 688136 | tf_op jit(solution)/shard_map/ppermute | solution.py:180
  24.9 3.5 %collective-permute-done.1.refs_2_ = bf16[16,7,8,128]{3,2,1,0:T(8,128)(2,1)S(1)} collective-permute-done((bf16[16,7,8,128]{3,2,1,0:T(8,128)(2,1)S(1)}, bf16[16,7,8,128]{3,2,1,0:T(8,128)(2,1)S(1)}, u32[]{:S(2)}, u32[]{:S(2)}) %collective-permute-start.1) | collective-permute-done | bytes 229408 | tf_op jit(solution)/shard_map/ppermute | solution.py:180
  28.5 3.7 %collective-permute-start.2 = (bf16[16,7,8,128]{3,2,1,0:T(8,128)(2,1)S(1)}, bf16[16,7,8,128]{3,2,1,0:T(8,128)(2,1)S(1)}, u32[]{:S(2)}, u32[]{:S(2)}) collective-permute-start(bf16[16,7,8,128]{3,2,1,0:T(8,128)(2,1)S(1)} %collective-permute-done.1.refs_2_), channel_id=1, source_target_pairs={{8,0},{16,8},{24,16},{32,24},{40,32},{48,40},{56,48},{0,56},{9,1},... | collective-permute-start | bytes 688136 | tf_op jit(solution)/shard_map/ppermute | solution.py:180
  32.2 0.3 collective-permute-done.5.refs_6_
  32.4 4.3 %collective-permute-done.2.refs_3_ = bf16[16,7,8,128]{3,2,1,0:T(8,128)(2,1)S(1)} collective-permute-done((bf16[16,7,8,128]{3,2,1,0:T(8,128)(2,1)S(1)}, bf16[16,7,8,128]{3,2,1,0:T(8,128)(2,1)S(1)}, u32[]{:S(2)}, u32[]{:S(2)}) %collective-permute-start.2) | collective-permute-done | bytes 229408 | tf_op jit(solution)/shard_map/ppermute | solution.py:180
  36.7 3.8 %collective-permute-start.3 = (bf16[8,7,8,128]{3,2,1,0:T(8,128)(2,1)S(1)}, bf16[8,7,8,128]{3,2,1,0:T(8,128)(2,1)S(1)}, u32[]{:S(2)}, u32[]{:S(2)}) collective-permute-start(bf16[8,7,8,128]{3,2,1,0:T(8,128)(2,1)S(1)} %slice.12), channel_id=1, source_target_pairs={{8,0},{16,8},{24,16},{32,24},{40,32},{48,40},{56,48},{0,56},{9,1},... | collective-permute-start | bytes 344072 | tf_op jit(solution)/shard_map/ppermute | solution.py:180
  40.5 0.5 collective-permute-start.15
  41.0 0.5 collective-permute-start.14
  41.5 1.3 %collective-permute-done.3 = bf16[8,7,8,128]{3,2,1,0:T(8,128)(2,1)S(1)} collective-permute-done((bf16[8,7,8,128]{3,2,1,0:T(8,128)(2,1)S(1)}, bf16[8,7,8,128]{3,2,1,0:T(8,128)(2,1)S(1)}, u32[]{:S(2)}, u32[]{:S(2)}) %collective-permute-start.3) | collective-permute-done | bytes 114720 | tf_op jit(solution)/shard_map/ppermute | solution.py:180
  42.9 6.4 %collective-permute-done.7 = bf16[8,7,8,128]{3,2,1,0:T(8,128)(2,1)S(1)} collective-permute-done((bf16[8,7,8,128]{3,2,1,0:T(8,128)(2,1)S(1)}, bf16[8,7,8,128]{3,2,1,0:T(8,128)(2,1)S(1)}, u32[]{:S(2)}, u32[]{:S(2)}) %collective-permute-start.7) | collective-permute-done | bytes 114720 | tf_op jit(solution)/shard_map/ppermute | solution.py:180
  49.3 0.6 collective-permute-start.13
  50.1 0.4 collective-permute-start.12
  50.6 0.8 reshape.9.lists
  51.4 0.7 pad_add_fusion.where
  52.2 0.5 copy-done.11
  52.9 8.4 %select.1 = bf16[16,57,8,128]{3,2,1,0:T(8,128)(2,1)} custom-call(s32[3328]{0:T(1024)} %reshape.9.lists, s32[4]{0:T(128)} %pad_add_fusion.where, bf16[16,7,8,128]{3,2,1,0:T(8,128)(2,1)} %bitcast.16, bf16[16,7,8,128]{3,2,1,0:T(8,128)(2,1)} %copy-done.4, bf16[16,7,8,128]{3,2,1,0:T(8,128)(2,1)} %copy-done.6, bf16[16,7,8,128]{3,2,1,0:T(8,128)(2,1)} %copy-done.1, ...), custom_call_target="tpu_custom_call" | custom-call | tf_op jit(solution)/shard_map/select/pallas_call | solution.py:83
  61.3 30.1 %all_to_all.16.got = bf16[16,57,8,128]{3,2,1,0:T(8,128)(2,1)} all-to-all(bf16[16,57,8,128]{3,2,1,0:T(8,128)(2,1)} %select.1), channel_id=1, replica_groups=mesh['x'=4,'z'=8,'core'=2,'y'=4] {'x','y'}, dimensions={0} | all-to-all | bytes 3735552 | tf_op jit(solution)/shard_map/all_to_all | solution.py:204
  91.4 5.3 %purify.1 = bf16[4,13,32,128]{3,2,1,0:T(8,128)(2,1)} custom-call(s32[3328]{0:T(1024)} %reshape.9.lists, s32[4]{0:T(128)} %pad_add_fusion.where, bf16[16,57,8,128]{3,2,1,0:T(8,128)(2,1)} %all_to_all.16.got, bf16[4,13,128,128]{3,2,1,0:T(8,128)(2,1)} %own.1), custom_call_target="tpu_custom_call" | custom-call | tf_op jit(solution)/shard_map/purify/pallas_call | solution.py:164
  96.7 11.3 %all_to_all.17 = bf16[4,13,32,128]{3,2,1,0:T(8,128)(2,1)S(1)} all-to-all(bf16[4,13,32,128]{3,2,1,0:T(8,128)(2,1)} %purify.1), channel_id=1, replica_groups=mesh['x'=4,'z'=8,'core'=2,'y'=4] {'y'}, dimensions={0} | all-to-all | bytes 851968 | tf_op jit(solution)/shard_map/all_to_all | solution.py:206
  107.9 0.8 copy.9
  (54 shorter events, 0.6 us)
Async XLA Ops:
  0.0 50.4 %copy-start.14 = (s32[256,13]{0,1:T(8,128)S(1)}, s32[256,13]{0,1:T(8,128)}, u32[]{:S(2)}) copy-start(s32[256,13]{0,1:T(8,128)} %param.2) | copy-start | bytes 39940
  11.8 40.3 %copy-start = (bf16[4,4,7,8,128]{4,3,2,1,0:T(8,128)(2,1)}, bf16[4,4,7,8,128]{4,3,2,1,0:T(8,128)(2,1)S(1)}, u32[]{:S(2)}) copy-start(bf16[4,4,7,8,128]{4,3,2,1,0:T(8,128)(2,1)S(1)} %all_to_all.15) | copy-start | bytes 688132
  11.8 9.4 %collective-permute-start = (bf16[16,7,8,128]{3,2,1,0:T(8,128)(2,1)S(1)}, bf16[16,7,8,128]{3,2,1,0:T(8,128)(2,1)S(1)}, u32[]{:S(2)}, u32[]{:S(2)}) collective-permute-start(bf16[16,7,8,128]{3,2,1,0:T(8,128)(2,1)S(1)} %bitcast.13), channel_id=1, source_target_pairs={{8,0},{16,8},{24,16},{32,24},{40,32},{48,40},{56,48},{0,56},{9,1},... | collective-permute-start | bytes 688136 | tf_op jit(solution)/shard_map/ppermute | solution.py:180
  17.7 7.2 %collective-permute-start.4 = (bf16[16,7,8,128]{3,2,1,0:T(8,128)(2,1)S(1)}, bf16[16,7,8,128]{3,2,1,0:T(8,128)(2,1)S(1)}, u32[]{:S(2)}, u32[]{:S(2)}) collective-permute-start(bf16[16,7,8,128]{3,2,1,0:T(8,128)(2,1)S(1)} %bitcast.14), channel_id=1, source_target_pairs={{56,0},{0,8},{8,16},{16,24},{24,32},{32,40},{40,48},{48,56},{57,1}... | collective-permute-start | bytes 688136 | tf_op jit(solution)/shard_map/ppermute | solution.py:180
  21.2 30.9 %copy-start.4 = (bf16[16,7,8,128]{3,2,1,0:T(8,128)(2,1)}, bf16[16,7,8,128]{3,2,1,0:T(8,128)(2,1)S(1)}, u32[]{:S(2)}) copy-start(bf16[16,7,8,128]{3,2,1,0:T(8,128)(2,1)S(1)} %collective-permute-done.refs_1_) | copy-start | bytes 688132
  21.2 7.2 %collective-permute-start.1 = (bf16[16,7,8,128]{3,2,1,0:T(8,128)(2,1)S(1)}, bf16[16,7,8,128]{3,2,1,0:T(8,128)(2,1)S(1)}, u32[]{:S(2)}, u32[]{:S(2)}) collective-permute-start(bf16[16,7,8,128]{3,2,1,0:T(8,128)(2,1)S(1)} %collective-permute-done.refs_1_), channel_id=1, source_target_pairs={{8,0},{16,8},{24,16},{32,24},{40,32},{48,40},{56,48},{0,56},{9,1},... | collective-permute-start | bytes 688136 | tf_op jit(solution)/shard_map/ppermute | solution.py:180
  24.9 27.2 %copy-start.5 = (bf16[16,7,8,128]{3,2,1,0:T(8,128)(2,1)}, bf16[16,7,8,128]{3,2,1,0:T(8,128)(2,1)S(1)}, u32[]{:S(2)}) copy-start(bf16[16,7,8,128]{3,2,1,0:T(8,128)(2,1)S(1)} %collective-permute-done.4.refs_7_) | copy-start | bytes 688132
  24.9 7.5 %collective-permute-start.5 = (bf16[16,7,8,128]{3,2,1,0:T(8,128)(2,1)S(1)}, bf16[16,7,8,128]{3,2,1,0:T(8,128)(2,1)S(1)}, u32[]{:S(2)}, u32[]{:S(2)}) collective-permute-start(bf16[16,7,8,128]{3,2,1,0:T(8,128)(2,1)S(1)} %collective-permute-done.4.refs_7_), channel_id=1, source_target_pairs={{56,0},{0,8},{8,16},{16,24},{24,32},{32,40},{40,48},{48,56},{57,1}... | collective-permute-start | bytes 688136 | tf_op jit(solution)/shard_map/ppermute | solution.py:180
  28.5 23.7 %copy-start.6 = (bf16[16,7,8,128]{3,2,1,0:T(8,128)(2,1)}, bf16[16,7,8,128]{3,2,1,0:T(8,128)(2,1)S(1)}, u32[]{:S(2)}) copy-start(bf16[16,7,8,128]{3,2,1,0:T(8,128)(2,1)S(1)} %collective-permute-done.1.refs_2_) | copy-start | bytes 688132
  28.5 8.3 %collective-permute-start.2 = (bf16[16,7,8,128]{3,2,1,0:T(8,128)(2,1)S(1)}, bf16[16,7,8,128]{3,2,1,0:T(8,128)(2,1)S(1)}, u32[]{:S(2)}, u32[]{:S(2)}) collective-permute-start(bf16[16,7,8,128]{3,2,1,0:T(8,128)(2,1)S(1)} %collective-permute-done.1.refs_2_), channel_id=1, source_target_pairs={{8,0},{16,8},{24,16},{32,24},{40,32},{48,40},{56,48},{0,56},{9,1},... | collective-permute-start | bytes 688136 | tf_op jit(solution)/shard_map/ppermute | solution.py:180
  32.4 19.7 %copy-start.7 = (bf16[16,7,8,128]{3,2,1,0:T(8,128)(2,1)}, bf16[16,7,8,128]{3,2,1,0:T(8,128)(2,1)S(1)}, u32[]{:S(2)}) copy-start(bf16[16,7,8,128]{3,2,1,0:T(8,128)(2,1)S(1)} %collective-permute-done.5.refs_6_) | copy-start | bytes 688132
  32.4 8.6 %collective-permute-start.6 = (bf16[16,7,8,128]{3,2,1,0:T(8,128)(2,1)S(1)}, bf16[16,7,8,128]{3,2,1,0:T(8,128)(2,1)S(1)}, u32[]{:S(2)}, u32[]{:S(2)}) collective-permute-start(bf16[16,7,8,128]{3,2,1,0:T(8,128)(2,1)S(1)} %collective-permute-done.5.refs_6_), channel_id=1, source_target_pairs={{56,0},{0,8},{8,16},{16,24},{24,32},{32,40},{40,48},{48,56},{57,1}... | collective-permute-start | bytes 688136 | tf_op jit(solution)/shard_map/ppermute | solution.py:180
  36.7 15.4 %copy-start.1 = (bf16[16,7,8,128]{3,2,1,0:T(8,128)(2,1)}, bf16[16,7,8,128]{3,2,1,0:T(8,128)(2,1)S(1)}, u32[]{:S(2)}) copy-start(bf16[16,7,8,128]{3,2,1,0:T(8,128)(2,1)S(1)} %collective-permute-done.2.refs_3_) | copy-start | bytes 688132
  36.7 6.1 %collective-permute-start.3 = (bf16[8,7,8,128]{3,2,1,0:T(8,128)(2,1)S(1)}, bf16[8,7,8,128]{3,2,1,0:T(8,128)(2,1)S(1)}, u32[]{:S(2)}, u32[]{:S(2)}) collective-permute-start(bf16[8,7,8,128]{3,2,1,0:T(8,128)(2,1)S(1)} %slice.12), channel_id=1, source_target_pairs={{8,0},{16,8},{24,16},{32,24},{40,32},{48,40},{56,48},{0,56},{9,1},... | collective-permute-start | bytes 344072 | tf_op jit(solution)/shard_map/ppermute | solution.py:180
  40.5 8.8 %collective-permute-start.8 = (bf16[16,7,8,128]{3,2,1,0:T(8,128)(2,1)S(1)}, bf16[16,7,8,128]{3,2,1,0:T(8,128)(2,1)S(1)}, u32[]{:S(2)}, u32[]{:S(2)}) collective-permute-start(bf16[16,7,8,128]{3,2,1,0:T(8,128)(2,1)S(1)} %bitcast.15), channel_id=1, source_target_pairs={{4,0},{0,4},{5,1},{1,5},{6,2},{2,6},{7,3},{3,7},{12,8},{8,12},{13,... | collective-permute-start | bytes 688136 | tf_op jit(solution)/shard_map/ppermute | solution.py:180
  40.5 9.4 %collective-permute-start.15 = (bf16[16,7,8,128]{3,2,1,0:T(8,128)(2,1)S(1)}, bf16[16,7,8,128]{3,2,1,0:T(8,128)(2,1)S(1)}, u32[]{:S(2)}, u32[]{:S(2)}) collective-permute-start(bf16[16,7,8,128]{3,2,1,0:T(8,128)(2,1)S(1)} %collective-permute-done.4.refs_7_), channel_id=1, source_target_pairs={{4,0},{0,4},{5,1},{1,5},{6,2},{2,6},{7,3},{3,7},{12,8},{8,12},{13,... | collective-permute-start | bytes 688136 | tf_op jit(solution)/shard_map/ppermute | solution.py:180
  41.0 9.0 %collective-permute-start.9 = (bf16[16,7,8,128]{3,2,1,0:T(8,128)(2,1)S(1)}, bf16[16,7,8,128]{3,2,1,0:T(8,128)(2,1)S(1)}, u32[]{:S(2)}, u32[]{:S(2)}) collective-permute-start(bf16[16,7,8,128]{3,2,1,0:T(8,128)(2,1)S(1)} %collective-permute-done.refs_1_), channel_id=1, source_target_pairs={{4,0},{0,4},{5,1},{1,5},{6,2},{2,6},{7,3},{3,7},{12,8},{8,12},{13,... | collective-permute-start | bytes 688136 | tf_op jit(solution)/shard_map/ppermute | solution.py:180
  41.0 11.1 %copy-start.2 = (bf16[16,7,8,128]{3,2,1,0:T(8,128)(2,1)}, bf16[16,7,8,128]{3,2,1,0:T(8,128)(2,1)S(1)}, u32[]{:S(2)}) copy-start(bf16[16,7,8,128]{3,2,1,0:T(8,128)(2,1)S(1)} %collective-permute-done.6.refs_5_) | copy-start | bytes 688132
  41.0 11.0 %collective-permute-start.14 = (bf16[16,7,8,128]{3,2,1,0:T(8,128)(2,1)S(1)}, bf16[16,7,8,128]{3,2,1,0:T(8,128)(2,1)S(1)}, u32[]{:S(2)}, u32[]{:S(2)}) collective-permute-start(bf16[16,7,8,128]{3,2,1,0:T(8,128)(2,1)S(1)} %collective-permute-done.5.refs_6_), channel_id=1, source_target_pairs={{4,0},{0,4},{5,1},{1,5},{6,2},{2,6},{7,3},{3,7},{12,8},{8,12},{13,... | collective-permute-start | bytes 688136 | tf_op jit(solution)/shard_map/ppermute | solution.py:180
  42.9 6.4 %collective-permute-start.7 = (bf16[8,7,8,128]{3,2,1,0:T(8,128)(2,1)S(1)}, bf16[8,7,8,128]{3,2,1,0:T(8,128)(2,1)S(1)}, u32[]{:S(2)}, u32[]{:S(2)}) collective-permute-start(bf16[8,7,8,128]{3,2,1,0:T(8,128)(2,1)S(1)} %slice.13), channel_id=1, source_target_pairs={{56,0},{0,8},{8,16},{16,24},{24,32},{32,40},{40,48},{48,56},{57,1}... | collective-permute-start | bytes 344072 | tf_op jit(solution)/shard_map/ppermute | solution.py:180
  49.3 2.8 %collective-permute-start.10 = (bf16[16,7,8,128]{3,2,1,0:T(8,128)(2,1)S(1)}, bf16[16,7,8,128]{3,2,1,0:T(8,128)(2,1)S(1)}, u32[]{:S(2)}, u32[]{:S(2)}) collective-permute-start(bf16[16,7,8,128]{3,2,1,0:T(8,128)(2,1)S(1)} %collective-permute-done.1.refs_2_), channel_id=1, source_target_pairs={{4,0},{0,4},{5,1},{1,5},{6,2},{2,6},{7,3},{3,7},{12,8},{8,12},{13,... | collective-permute-start | bytes 688136 | tf_op jit(solution)/shard_map/ppermute | solution.py:180
  49.3 2.7 %collective-permute-start.13 = (bf16[16,7,8,128]{3,2,1,0:T(8,128)(2,1)S(1)}, bf16[16,7,8,128]{3,2,1,0:T(8,128)(2,1)S(1)}, u32[]{:S(2)}, u32[]{:S(2)}) collective-permute-start(bf16[16,7,8,128]{3,2,1,0:T(8,128)(2,1)S(1)} %collective-permute-done.6.refs_5_), channel_id=1, source_target_pairs={{4,0},{0,4},{5,1},{1,5},{6,2},{2,6},{7,3},{3,7},{12,8},{8,12},{13,... | collective-permute-start | bytes 688136 | tf_op jit(solution)/shard_map/ppermute | solution.py:180
  49.9 2.1 %collective-permute-start.11 = (bf16[16,7,8,128]{3,2,1,0:T(8,128)(2,1)S(1)}, bf16[16,7,8,128]{3,2,1,0:T(8,128)(2,1)}, u32[]{:S(2)}, u32[]{:S(2)}) collective-permute-start(bf16[16,7,8,128]{3,2,1,0:T(8,128)(2,1)S(1)} %collective-permute-done.2.refs_3_), channel_id=1, source_target_pairs={{4,0},{0,4},{5,1},{1,5},{6,2},{2,6},{7,3},{3,7},{12,8},{8,12},{13,... | collective-permute-start | bytes 688136 | tf_op jit(solution)/shard_map/ppermute | solution.py:180
  50.1 2.0 %collective-permute-start.12 = (bf16[16,7,8,128]{3,2,1,0:T(8,128)(2,1)S(1)}, bf16[16,7,8,128]{3,2,1,0:T(8,128)(2,1)}, u32[]{:S(2)}, u32[]{:S(2)}) collective-permute-start(bf16[16,7,8,128]{3,2,1,0:T(8,128)(2,1)S(1)} %constant_dynamic-update-slice_fusion.refs_4_), channel_id=1, source_target_pairs={{4,0},{0,4},{5,1},{1,5},{6,2},{2,6},{7,3},{3,7},{12,8},{8,12},{13,... | collective-permute-start | bytes 688136 | tf_op jit(solution)/shard_map/ppermute | solution.py:180
  (8 other events, 13.6 us)

commit v2 on v1

v2 whole, which is shorter than its diff:
```python
import jax
import jax.numpy as jnp
from jax import lax
from jax.experimental import pallas as pl
from jax.experimental.pallas import tpu as pltpu
from jax.sharding import Mesh
from jax.sharding import PartitionSpec as P

X, ZL, ZP, CORE, Y = 4, 4, 2, 2, 4
Z = ZL * ZP
BLK = 128
SLOTS = 13
MID = 6
HALF = 7
ROWS_HERE = 4
TILES = X * Y
TILE = BLK // TILES
DESTS = X * ZP * Y
OWNERS = X * Z
CLASSES = ((0, 2, 4, 6), (1, 3, 5, 6))
USED = ((0, 2, 4), (1, 3, 5, 6))
DEPTH = 4
AXES = ("x", "zl", "zp", "core", "y")


def wanted(cls):
    return [
        (a, a + d) for a in range(SLOTS) for d in USED[cls] if a != MID and a + d != MID and a + d < SLOTS
    ]


WANTED = (wanted(0), wanted(1))
COUNT = max(len(w) for w in WANTED)


def runs(cls):
    out = {}
    for place, (a, s) in enumerate(WANTED[cls]):
        j = CLASSES[cls].index(s - a)
        mine = out.setdefault(a, [])
        if mine and mine[-1][0] + mine[-1][1] == j:
            mine[-1][1] += 1
        else:
            mine.append([j, 1, place])
    return list(out.items())


SMEM = pl.BlockSpec(memory_space=pltpu.SMEM)
ANY = pl.BlockSpec(memory_space=pl.ANY)


def pack_kernel(values, out, stage, sems, out_sems):
    y = lax.axis_index("y")
    copies = []
    for x in range(X):
        for zp in range(ZP):
            for j, d in enumerate(CLASSES[zp]):
                rows = pl.ds(pl.multiple_of((x * Y + y) * TILE, TILE), TILE)
                n = len(copies)
                copies.append(
                    pltpu.make_async_copy(values.at[:, MID + d, rows], stage.at[x, zp, :, j], sems.at[n])
                )
    for copy in copies:
        copy.start()
    for copy in copies:
        copy.wait()
    copies = [pltpu.make_async_copy(stage, out.at[:, zl], out_sems.at[zl]) for zl in range(ZL)]
    for copy in copies:
        copy.start()
    for copy in copies:
        copy.wait()


def pack(values):
    shape = (X, ZP, ROWS_HERE, DEPTH, TILE, BLK)
    return pl.pallas_call(
        pack_kernel,
        out_shape=jax.ShapeDtypeStruct((X, ZL) + shape[1:], jnp.bfloat16),
        in_specs=[ANY],
        out_specs=ANY,
        scratch_shapes=[
            pltpu.VMEM(shape, jnp.bfloat16),
            pltpu.SemaphoreType.DMA((X * ZP * DEPTH,)),
            pltpu.SemaphoreType.DMA((ZL,)),
        ],
        name="pack",
    )(values)


def select_kernel(lists, here, there, out, held, sems):
    zl, zp, core = (lax.axis_index(a) for a in ("zl", "zp", "core"))
    copies = [
        pltpu.make_async_copy(here, held.at[core], sems.at[0]),
        pltpu.make_async_copy(there, held.at[1 - core], sems.at[1]),
    ]
    for copy in copies:
        copy.start()
    for copy in copies:
        copy.wait()

    def run(cls):
        def one(t, carry):
            owner = ((t // (ZP * Y)) * Z + 2 * zl + lax.rem(t // Y, ZP)) * CORE + core
            row = ROWS_HERE * owner + lax.rem(t, Y)
            for a, parts in runs(cls):
                k = jnp.maximum(lists[a, row], 0)
                k_core = lax.rem(k // ROWS_HERE, CORE)
                k_owner = k // (ROWS_HERE * CORE)
                k_row = lax.rem(k, ROWS_HERE)
                for j, length, place in parts:
                    out[t, place : place + length] = held[k_core, k_owner, k_row, j : j + length]
            return carry

        lax.fori_loop(0, DESTS, one, 0)

    pl.when(zp == 0)(lambda: run(0))
    pl.when(zp == 1)(lambda: run(1))


def select(lists, here, there):
    return pl.pallas_call(
        select_kernel,
        out_shape=jax.ShapeDtypeStruct((DESTS, COUNT, TILE, BLK), jnp.bfloat16),
        in_specs=[SMEM, ANY, ANY],
        out_specs=pl.BlockSpec(memory_space=pltpu.VMEM),
        scratch_shapes=[
            pltpu.VMEM((CORE, OWNERS, ROWS_HERE, DEPTH, TILE, BLK), jnp.bfloat16),
            pltpu.SemaphoreType.DMA((2,)),
        ],
        name="select",
    )(lists, here, there)


def groups():
    out = []
    for s in range(0, SLOTS, 2):
        n = min(2, SLOTS - s)
        low = max(0, s - MID)
        high = min(SLOTS - 1, s + n - 1 + MID)
        out.append((s, n, low, high - low + 1))
    return out


GROUPS = groups()


def purify_kernel(lists, got, own, out, u, w, sq, sems):
    x, zl, zp, core, y = (lax.axis_index(a) for a in AXES)
    row = ROWS_HERE * ((x * Z + 2 * zl + zp) * CORE + core) + y
    copies = []
    for p in range(DESTS):
        tile = (p // (ZP * Y)) * Y + p % Y
        copies.append(pltpu.make_async_copy(got.at[p], u.at[(p // Y) % ZP, :, tile], sems.at[p]))
    for s in range(SLOTS):
        copies.append(
            pltpu.make_async_copy(
                own.at[y, s],
                w.at[MID * BLK : (MID + 1) * BLK, s * BLK : (s + 1) * BLK],
                sems.at[DESTS + s],
            )
        )
    for copy in copies:
        copy.start()

    def blk(a):
        return slice(a * BLK, (a + 1) * BLK)

    for a in range(SLOTS - HALF):
        w[blk(a), blk(a + HALF)] = jnp.zeros((BLK, BLK), jnp.bfloat16)
        w[blk(a + HALF), blk(a)] = jnp.zeros((BLK, BLK), jnp.bfloat16)
    for copy in copies:
        copy.wait()
    for s in range(SLOTS):
        if s != MID:
            w[blk(s), blk(MID)] = w[blk(MID), blk(s)].T
    for cls in range(ZP):
        for place, (a, s) in enumerate(WANTED[cls]):
            value = u[cls, place].reshape(BLK, BLK)
            w[blk(a), blk(s)] = value
            if a != s:
                w[blk(s), blk(a)] = value.T

    def mask(value, s):
        return jnp.where(lists[s, row] >= 0, value, jnp.zeros_like(value))

    def span(first, n):
        return slice(first * BLK, (first + n) * BLK)

    for s, n, low, count in GROUPS:
        total = jnp.dot(
            w[blk(MID), span(low, count)], w[span(low, count), span(s, n)], preferred_element_type=jnp.float32
        )
        for j in range(n):
            sq[:, blk(s + j)] = mask(total[:, blk(j)], s + j).astype(jnp.bfloat16)
    for s, n, low, count in GROUPS:
        total = jnp.dot(sq[:, span(low, count)], w[span(low, count), span(s, n)], preferred_element_type=jnp.float32)
        for j in range(n):
            value = 3.0 * sq[:, blk(s + j)].astype(jnp.float32) - 2.0 * total[:, blk(j)]
            value = mask(value, s + j).T.astype(jnp.bfloat16)
            for part in range(Y):
                out[part, s + j] = value[part * (BLK // Y) : (part + 1) * (BLK // Y)]


def purify(lists, got, own):
    return pl.pallas_call(
        purify_kernel,
        out_shape=jax.ShapeDtypeStruct((Y, SLOTS, BLK // Y, BLK), jnp.bfloat16),
        in_specs=[SMEM, ANY, ANY],
        out_specs=pl.BlockSpec(memory_space=pltpu.VMEM),
        scratch_shapes=[
            pltpu.VMEM((ZP, COUNT, TILES, TILE, BLK), jnp.bfloat16),
            pltpu.VMEM((SLOTS * BLK, SLOTS * BLK), jnp.bfloat16),
            pltpu.VMEM((BLK, SLOTS * BLK), jnp.bfloat16),
            pltpu.SemaphoreType.DMA((DESTS + SLOTS,)),
        ],
        name="purify",
    )(lists, got, own)


def body(column_lists, block_values):
    lists = column_lists.T
    mine = pack(block_values).reshape(OWNERS, ROWS_HERE, DEPTH, TILE, BLK)
    here = lax.all_to_all(mine, ("x", "zl", "zp"), 0, 0, tiled=True)
    there = lax.ppermute(here, "core", [(0, 1), (1, 0)])
    asked = select(lists, here, there)
    got = lax.all_to_all(asked, ("x", "zp", "y"), 0, 0, tiled=True)
    strips = purify(lists, got, block_values)
    mixed = lax.all_to_all(strips, "y", 0, 0, tiled=True)
    return mixed.transpose(0, 1, 3, 2)


def solution(mesh):
    fine = Mesh(mesh.devices.reshape(X, ZL, ZP, CORE, Y), AXES)
    rows = ("x", "zl", "zp", "core")
    return jax.shard_map(
        body, mesh=fine, in_specs=(P(), P(rows)), out_specs=P(rows, None, None, "y"), check_vma=False
    )
```

time: 109 us -> 103 us (0.945)
  blocking collectives: 51.9 us -> 83.1 us
  starting transfers between devices: 19.2 us -> 0.01 us
  waiting for transfers between devices: 19.4 us -> 2.66 us
  local copies, waits for them, and re-layouts: 3.69 us -> 1.72 us
  Pallas kernels: 13.7 us -> 15.2 us
    all_to_all x2, blocking collectives: 40.7 us -> 72.7 us  [the longest x1 40 us: body(): here = lax.all_to_all(mine, ('x', 'zl', 'zp'), 0, 0, tiled=True)]
    ppermute x16 -> x1, starting transfers between devices: 19.2 us -> 0.01 us  [body(): there = lax.ppermute(here, 'core', [(0, 1), (1, 0)])]
    ppermute x16 -> x1, waiting for transfers between devices: 19.4 us -> 2.66 us  [body(): there = lax.ppermute(here, 'core', [(0, 1), (1, 0)])]
    pallas_call x1 -> x2, Pallas kernels: 8.37 us -> 9.74 us  [the longest x1 7.5 us: select(): pl.pallas_call(select_kernel, out_shape=jax.ShapeDtypeStruct((DESTS, COUN...]
    slice x4 -> x0, local copies, waits for them, and re-layouts: 1.2 us -> none  [the longest x2 1.18 us: body(): tiles = block_values[:, MID:].reshape(ROWS_HERE, HALF, X, Y, TILE, BLK)]
  transfers between devices with their start and end apart: 16 -> 1, of which waited for: 6 -> 1; matrix products, arithmetic and copies ran while one was open for 1% -> 0% of each run, Pallas kernels for 0% -> 0%
where the time goes in v2:
time: 103 us
  blocking collectives  83.1 us (81%)
  Pallas kernels  15.2 us (15%)
  waiting for transfers between devices  2.66 us (3%)
  local copies, waits for them, and re-layouts  1.72 us (2%)
    all_to_all x1, blocking collectives, body(): here = lax.all_to_all(mine, ('x', 'zl', 'zp'), 0, 0, tiled=True)  40 us
    all_to_all x1, blocking collectives, body(): got = lax.all_to_all(asked, ('x', 'zp', 'y'), 0, 0, tiled=True)  32.8 us
    all_to_all x1, blocking collectives, body(): mixed = lax.all_to_all(strips, 'y', 0, 0, tiled=True)  10.4 us
    pallas_call x1, Pallas kernels, select(): pl.pallas_call(select_kernel, out_shape=jax.ShapeDtypeStruct((DESTS, COUN...  7.5 us
    pallas_call x1, Pallas kernels, purify(): pl.pallas_call(purify_kernel, out_shape=jax.ShapeDtypeStruct((Y, SLOTS, B...  5.47 us
    ppermute x1, waiting for transfers between devices, body(): there = lax.ppermute(here, 'core', [(0, 1), (1, 0)])  2.66 us
    pallas_call x1, Pallas kernels, pack(): pl.pallas_call(pack_kernel, out_shape=jax.ShapeDtypeStruct((X, ZL) + shap...  2.25 us
  transfers between devices with their start and end apart: 1, of which 1 were waited for; matrix products, arithmetic and copies ran while one was open for 0% of the time, Pallas kernels for 0%

profile of v2, /device:TPU:8, one launch (start us, length us, event | category | flops | bytes accessed | tf_op | source)
XLA Modules:
  0.0 102.7 jit_solution(16622167328494899657)
XLA Ops:
  0.0 2.2 %pack.1 = bf16[4,4,2,4,4,8,128]{6,5,4,3,2,1,0:T(8,128)(2,1)} custom-call(bf16[4,13,128,128]{3,2,1,0:T(8,128)(2,1)} %own.1), custom_call_target="tpu_custom_call" | custom-call | tf_op jit(solution)/shard_map/pack/pallas_call | solution.py:76
  2.3 40.0 %all_to_all.15.here = bf16[32,4,4,8,128]{4,3,2,1,0:T(8,128)(2,1)S(1)} all-to-all(bf16[32,4,4,8,128]{4,3,2,1,0:T(8,128)(2,1)} %bitcast.3), channel_id=1, replica_groups=mesh['x'=4,'zl'=4,'zp'=2,'core'=2,'y'=4] {'x','zl','zp'}, dimensions={0} | all-to-all | bytes 2097152 | tf_op jit(solution)/shard_map/all_to_all | solution.py:223
  42.2 0.0 copy-start
  42.2 0.0 collective-permute-start
  42.2 2.7 %collective-permute-done.there = bf16[32,4,4,8,128]{4,3,2,1,0:T(8,128)(2,1)S(1)} collective-permute-done((bf16[32,4,4,8,128]{4,3,2,1,0:T(8,128)(2,1)S(1)}, bf16[32,4,4,8,128]{4,3,2,1,0:T(8,128)(2,1)S(1)}, u32[]{:S(2)}, u32[]{:S(2)}) %collective-permute-start) | collective-permute-done | bytes 1048608 | tf_op jit(solution)/shard_map/ppermute | solution.py:224
  44.9 0.0 copy-start.1
  44.9 0.0 copy-done
  44.9 1.0 copy-done.1
  45.8 7.5 %select.1 = bf16[32,29,8,128]{3,2,1,0:T(8,128)(2,1)} custom-call(s32[13,256]{1,0:T(8,128)} %bitcast.5, bf16[32,4,4,8,128]{4,3,2,1,0:T(8,128)(2,1)} %copy-done, bf16[32,4,4,8,128]{4,3,2,1,0:T(8,128)(2,1)} %copy-done.1), custom_call_target="tpu_custom_call" | custom-call | tf_op jit(solution)/shard_map/select/pallas_call | solution.py:121
  53.4 32.8 %all_to_all.16.got = bf16[32,29,8,128]{3,2,1,0:T(8,128)(2,1)} all-to-all(bf16[32,29,8,128]{3,2,1,0:T(8,128)(2,1)} %select.1), channel_id=1, replica_groups=mesh['x'=4,'zl'=4,'zp'=2,'core'=2,'y'=4] {'x','zp','y'}, dimensions={0} | all-to-all | bytes 3801088 | tf_op jit(solution)/shard_map/all_to_all | solution.py:226
  86.1 5.5 %purify.1 = bf16[4,13,32,128]{3,2,1,0:T(8,128)(2,1)} custom-call(s32[13,256]{1,0:T(8,128)} %bitcast.6, bf16[32,29,8,128]{3,2,1,0:T(8,128)(2,1)} %all_to_all.16.got, bf16[4,13,128,128]{3,2,1,0:T(8,128)(2,1)} %own.1), custom_call_target="tpu_custom_call" | custom-call | tf_op jit(solution)/shard_map/purify/pallas_call | solution.py:205
  91.6 10.4 %all_to_all.17 = bf16[4,13,32,128]{3,2,1,0:T(8,128)(2,1)S(1)} all-to-all(bf16[4,13,32,128]{3,2,1,0:T(8,128)(2,1)} %purify.1), channel_id=1, replica_groups=mesh['x'=4,'zl'=4,'zp'=2,'core'=2,'y'=4] {'y'}, dimensions={0} | all-to-all | bytes 851968 | tf_op jit(solution)/shard_map/all_to_all | solution.py:228
  101.9 0.8 copy.4
Async XLA Ops:
  42.2 2.7 %copy-start = (bf16[32,4,4,8,128]{4,3,2,1,0:T(8,128)(2,1)}, bf16[32,4,4,8,128]{4,3,2,1,0:T(8,128)(2,1)S(1)}, u32[]{:S(2)}) copy-start(bf16[32,4,4,8,128]{4,3,2,1,0:T(8,128)(2,1)S(1)} %all_to_all.15.here) | copy-start | bytes 3145732
  42.2 2.7 %collective-permute-start = (bf16[32,4,4,8,128]{4,3,2,1,0:T(8,128)(2,1)S(1)}, bf16[32,4,4,8,128]{4,3,2,1,0:T(8,128)(2,1)S(1)}, u32[]{:S(2)}, u32[]{:S(2)}) collective-permute-start(bf16[32,4,4,8,128]{4,3,2,1,0:T(8,128)(2,1)S(1)} %all_to_all.15.here), channel_id=1, source_target_pairs={{0,4},{4,0},{1,5},{5,1},{2,6},{6,2},{3,7},{7,3},{8,12},{12,8},{9,1... | collective-permute-start | bytes 3145736 | tf_op jit(solution)/shard_map/ppermute | solution.py:224
  44.9 1.0 copy-start.1

commit v3 on v2

--- a/solution.py
+++ b/solution.py
@@ -47,6 +47,12 @@
 
 SMEM = pl.BlockSpec(memory_space=pltpu.SMEM)
 ANY = pl.BlockSpec(memory_space=pl.ANY)
+VMEM = pl.BlockSpec(memory_space=pltpu.VMEM)
+MIB = 1 << 20
+
+
+def near(value):
+    return pltpu.with_memory_space_constraint(value, pltpu.VMEM)
 
 
 def pack_kernel(values, out, stage, sems, out_sems):
@@ -75,28 +81,31 @@
     shape = (X, ZP, ROWS_HERE, DEPTH, TILE, BLK)
     return pl.pallas_call(
         pack_kernel,
-        out_shape=jax.ShapeDtypeStruct((X, ZL) + shape[1:], jnp.bfloat16),
+        out_shape=pltpu.VMEM((X, ZL) + shape[1:], jnp.bfloat16),
         in_specs=[ANY],
-        out_specs=ANY,
+        out_specs=VMEM,
         scratch_shapes=[
             pltpu.VMEM(shape, jnp.bfloat16),
             pltpu.SemaphoreType.DMA((X * ZP * DEPTH,)),
             pltpu.SemaphoreType.DMA((ZL,)),
         ],
+        compiler_params=pltpu.CompilerParams(vmem_limit_bytes=4 * MIB),
         name="pack",
-    )(values)
+    )(pltpu.with_memory_space_constraint(values, pltpu.HBM))
 
 
 def select_kernel(lists, here, there, out, held, sems):
     zl, zp, core = (lax.axis_index(a) for a in ("zl", "zp", "core"))
     copies = [
-        pltpu.make_async_copy(here, held.at[core], sems.at[0]),
-        pltpu.make_async_copy(there, held.at[1 - core], sems.at[1]),
+        pltpu.make_async_copy(here, held.at[:, core], sems.at[0]),
+        pltpu.make_async_copy(there, held.at[:, 1 - core], sems.at[1]),
     ]
     for copy in copies:
         copy.start()
     for copy in copies:
         copy.wait()
+
+    rows = held.reshape(OWNERS * CORE * ROWS_HERE, DEPTH, TILE, BLK)
 
     def run(cls):
         def one(t, carry):
@@ -104,11 +113,8 @@
             row = ROWS_HERE * owner + lax.rem(t, Y)
             for a, parts in runs(cls):
                 k = jnp.maximum(lists[a, row], 0)
-                k_core = lax.rem(k // ROWS_HERE, CORE)
-                k_owner = k // (ROWS_HERE * CORE)
-                k_row = lax.rem(k, ROWS_HERE)
                 for j, length, place in parts:
-                    out[t, place : place + length] = held[k_core, k_owner, k_row, j : j + length]
+                    out[t, place : place + length] = rows[k, j : j + length]
             return carry
 
         lax.fori_loop(0, DESTS, one, 0)
@@ -120,15 +126,16 @@
 def select(lists, here, there):
     return pl.pallas_call(
         select_kernel,
-        out_shape=jax.ShapeDtypeStruct((DESTS, COUNT, TILE, BLK), jnp.bfloat16),
-        in_specs=[SMEM, ANY, ANY],
-        out_specs=pl.BlockSpec(memory_space=pltpu.VMEM),
+        out_shape=pltpu.VMEM((DESTS, COUNT, TILE, BLK), jnp.bfloat16),
+        in_specs=[SMEM, VMEM, VMEM],
+        out_specs=VMEM,
         scratch_shapes=[
-            pltpu.VMEM((CORE, OWNERS, ROWS_HERE, DEPTH, TILE, BLK), jnp.bfloat16),
+            pltpu.VMEM((OWNERS, CORE, ROWS_HERE, DEPTH, TILE, BLK), jnp.bfloat16),
             pltpu.SemaphoreType.DMA((2,)),
         ],
+        compiler_params=pltpu.CompilerParams(vmem_limit_bytes=12 * MIB),
         name="select",
-    )(lists, here, there)
+    )(lists, near(here), near(there))
 
 
 def groups():
@@ -204,17 +211,18 @@
 def purify(lists, got, own):
     return pl.pallas_call(
         purify_kernel,
-        out_shape=jax.ShapeDtypeStruct((Y, SLOTS, BLK // Y, BLK), jnp.bfloat16),
-        in_specs=[SMEM, ANY, ANY],
-        out_specs=pl.BlockSpec(memory_space=pltpu.VMEM),
+        out_shape=pltpu.VMEM((Y, SLOTS, BLK // Y, BLK), jnp.bfloat16),
+        in_specs=[SMEM, VMEM, ANY],
+        out_specs=VMEM,
         scratch_shapes=[
             pltpu.VMEM((ZP, COUNT, TILES, TILE, BLK), jnp.bfloat16),
             pltpu.VMEM((SLOTS * BLK, SLOTS * BLK), jnp.bfloat16),
             pltpu.VMEM((BLK, SLOTS * BLK), jnp.bfloat16),
             pltpu.SemaphoreType.DMA((DESTS + SLOTS,)),
         ],
+        compiler_params=pltpu.CompilerParams(vmem_limit_bytes=24 * MIB),
         name="purify",
-    )(lists, got, own)
+    )(lists, near(got), own)
 
 
 def body(column_lists, block_values):

time: 103 us -> 93.8 us (0.911)
  Pallas kernels: 15.2 us -> 7.33 us
    pallas_call x3, Pallas kernels: 15.2 us -> 7.33 us  [the longest x1 3.78 us: purify(): pl.pallas_call(purify_kernel, out_shape=pltpu.VMEM((Y, SLOTS, BLK // Y, B...]
where the time goes in v3:
time: 93.8 us; the launch traced here: 93.5 us
  blocking collectives  82.7 us (88%)
  Pallas kernels  7.33 us (8%)
  waiting for transfers between devices  2.66 us (3%)
    all_to_all x1, blocking collectives, body(): here = lax.all_to_all(mine, ('x', 'zl', 'zp'), 0, 0, tiled=True)  39.8 us
    all_to_all x1, blocking collectives, body(): got = lax.all_to_all(asked, ('x', 'zp', 'y'), 0, 0, tiled=True)  32.8 us
    all_to_all x1, blocking collectives, body(): mixed = lax.all_to_all(strips, 'y', 0, 0, tiled=True)  10.1 us
    pallas_call x1, Pallas kernels, purify(): pl.pallas_call(purify_kernel, out_shape=pltpu.VMEM((Y, SLOTS, BLK // Y, B...  3.78 us
    ppermute x1, waiting for transfers between devices, body(): there = lax.ppermute(here, 'core', [(0, 1), (1, 0)])  2.66 us
    pallas_call x1, Pallas kernels, select(): pl.pallas_call(select_kernel, out_shape=pltpu.VMEM((DESTS, COUNT, TILE, B...  2.25 us
  transfers between devices with their start and end apart: 1, of which 1 were waited for; matrix products, arithmetic and copies ran while one was open for 0% of the time, Pallas kernels for 0%

profile of v3, /device:TPU:8, one launch (start us, length us, event | category | flops | bytes accessed | tf_op | source)
XLA Modules:
  0.0 93.5 jit_solution(9781678772961101081)
XLA Ops:
  0.0 0.0 copy-start.1
  0.0 1.3 %pack.1 = bf16[4,4,2,4,4,8,128]{6,5,4,3,2,1,0:T(8,128)(2,1)S(1)} custom-call(bf16[4,13,128,128]{3,2,1,0:T(8,128)(2,1)} %own.1), custom_call_target="tpu_custom_call" | custom-call | tf_op jit(solution)/shard_map/pack/pallas_call | solution.py:82
  1.3 39.8 %all_to_all.15.here = bf16[32,4,4,8,128]{4,3,2,1,0:T(8,128)(2,1)S(1)} all-to-all(bf16[32,4,4,8,128]{4,3,2,1,0:T(8,128)(2,1)S(1)} %bitcast.3), channel_id=1, replica_groups=mesh['x'=4,'zl'=4,'zp'=2,'core'=2,'y'=4] {'x','zl','zp'}, dimensions={0} | all-to-all | bytes 2097152 | tf_op jit(solution)/shard_map/all_to_all | solution.py:231
  41.1 0.0 collective-permute-start
  41.1 2.7 %collective-permute-done.there = bf16[32,4,4,8,128]{4,3,2,1,0:T(8,128)(2,1)S(1)} collective-permute-done((bf16[32,4,4,8,128]{4,3,2,1,0:T(8,128)(2,1)S(1)}, bf16[32,4,4,8,128]{4,3,2,1,0:T(8,128)(2,1)S(1)}, u32[]{:S(2)}, u32[]{:S(2)}) %collective-permute-start) | collective-permute-done | bytes 1048608 | tf_op jit(solution)/shard_map/ppermute | solution.py:232
  43.7 0.0 copy-done.1
  43.7 2.2 %select.1 = bf16[32,29,8,128]{3,2,1,0:T(8,128)(2,1)S(1)} custom-call(s32[13,256]{1,0:T(8,128)S(1)} %bitcast.4, bf16[32,4,4,8,128]{4,3,2,1,0:T(8,128)(2,1)S(1)} %all_to_all.15.here, bf16[32,4,4,8,128]{4,3,2,1,0:T(8,128)(2,1)S(1)} %collective-permute-done.there), custom_call_target="tpu_custom_call" | custom-call | tf_op jit(solution)/shard_map/select/pallas_call | solution.py:127
  46.0 0.0 copy-start
  46.0 32.8 %all_to_all.16.got = bf16[32,29,8,128]{3,2,1,0:T(8,128)(2,1)S(1)} all-to-all(bf16[32,29,8,128]{3,2,1,0:T(8,128)(2,1)S(1)} %select.1), channel_id=1, replica_groups=mesh['x'=4,'zl'=4,'zp'=2,'core'=2,'y'=4] {'x','zp','y'}, dimensions={0} | all-to-all | bytes 3801088 | tf_op jit(solution)/shard_map/all_to_all | solution.py:234
  78.8 0.0 copy-done
  78.8 3.8 %purify.1 = bf16[4,13,32,128]{3,2,1,0:T(8,128)(2,1)S(1)} custom-call(s32[13,256]{1,0:T(8,128)S(1)} %bitcast.5, bf16[32,29,8,128]{3,2,1,0:T(8,128)(2,1)S(1)} %all_to_all.16.got, bf16[4,13,128,128]{3,2,1,0:T(8,128)(2,1)S(1)} %copy-done), custom_call_target="tpu_custom_call" | custom-call | tf_op jit(solution)/shard_map/purify/pallas_call | solution.py:212
  82.6 10.1 %all_to_all.17 = bf16[4,13,32,128]{3,2,1,0:T(8,128)(2,1)S(1)} all-to-all(bf16[4,13,32,128]{3,2,1,0:T(8,128)(2,1)S(1)} %purify.1), channel_id=1, replica_groups=mesh['x'=4,'zl'=4,'zp'=2,'core'=2,'y'=4] {'y'}, dimensions={0} | all-to-all | bytes 851968 | tf_op jit(solution)/shard_map/all_to_all | solution.py:236
  92.8 0.8 copy.4
Async XLA Ops:
  0.0 43.7 %copy-start.1 = (s32[256,13]{0,1:T(8,128)S(1)}, s32[256,13]{0,1:T(8,128)}, u32[]{:S(2)}) copy-start(s32[256,13]{0,1:T(8,128)} %param.2) | copy-start | bytes 39940
  41.1 2.7 %collective-permute-start = (bf16[32,4,4,8,128]{4,3,2,1,0:T(8,128)(2,1)S(1)}, bf16[32,4,4,8,128]{4,3,2,1,0:T(8,128)(2,1)S(1)}, u32[]{:S(2)}, u32[]{:S(2)}) collective-permute-start(bf16[32,4,4,8,128]{4,3,2,1,0:T(8,128)(2,1)S(1)} %all_to_all.15.here), channel_id=1, source_target_pairs={{0,4},{4,0},{1,5},{5,1},{2,6},{6,2},{3,7},{7,3},{8,12},{12,8},{9,1... | collective-permute-start | bytes 3145736 | tf_op jit(solution)/shard_map/ppermute | solution.py:232
  46.0 32.9 %copy-start = (bf16[4,13,128,128]{3,2,1,0:T(8,128)(2,1)S(1)}, bf16[4,13,128,128]{3,2,1,0:T(8,128)(2,1)}, u32[]{:S(2)}) copy-start(bf16[4,13,128,128]{3,2,1,0:T(8,128)(2,1)} %own.1) | copy-start | bytes 5111812

commit v4 on v3

--- a/solution.py
+++ b/solution.py
@@ -17,32 +17,33 @@
 TILE = BLK // TILES
 DESTS = X * ZP * Y
 OWNERS = X * Z
-CLASSES = ((0, 2, 4, 6), (1, 3, 5, 6))
-USED = ((0, 2, 4), (1, 3, 5, 6))
-DEPTH = 4
+CLASSES = ((1, 4, 6), (2, 3, 5))
+DEPTH = 3
+FULL = DEPTH * ROWS_HERE
+MESSAGE = FULL + ROWS_HERE // 2
 AXES = ("x", "zl", "zp", "core", "y")
 
 
 def wanted(cls):
     return [
-        (a, a + d) for a in range(SLOTS) for d in USED[cls] if a != MID and a + d != MID and a + d < SLOTS
+        (a, a + d) for a in range(SLOTS) for d in CLASSES[cls] if a != MID and a + d != MID and a + d < SLOTS
     ]
 
 
 WANTED = (wanted(0), wanted(1))
-COUNT = max(len(w) for w in WANTED)
-
-
-def runs(cls):
-    out = {}
-    for place, (a, s) in enumerate(WANTED[cls]):
-        j = CLASSES[cls].index(s - a)
-        mine = out.setdefault(a, [])
-        if mine and mine[-1][0] + mine[-1][1] == j:
-            mine[-1][1] += 1
-        else:
-            mine.append([j, 1, place])
-    return list(out.items())
+DIAGONAL = [a for a in range(SLOTS) if a != MID]
+BASE = max(len(w) for w in WANTED)
+COUNT = BASE + len(DIAGONAL) // 2
+LANES = BLK // 2
+
+
+def turned(value):
+    return jnp.concatenate([value[:, LANES:], value[:, :LANES]], axis=1)
+
+
+def joined(left, right):
+    lane = lax.broadcasted_iota(jnp.int32, left.shape, 1)
+    return jnp.where(lane < LANES, left, right)
 
 
 SMEM = pl.BlockSpec(memory_space=pltpu.SMEM)
@@ -55,21 +56,26 @@
     return pltpu.with_memory_space_constraint(value, pltpu.VMEM)
 
 
-def pack_kernel(values, out, stage, sems, out_sems):
+def pack_kernel(values, out, stage, diagonal, sems, out_sems):
     y = lax.axis_index("y")
     copies = []
     for x in range(X):
+        rows = pl.ds(pl.multiple_of((x * Y + y) * TILE, TILE), TILE)
+        targets = [(0, diagonal.at[x])]
         for zp in range(ZP):
             for j, d in enumerate(CLASSES[zp]):
-                rows = pl.ds(pl.multiple_of((x * Y + y) * TILE, TILE), TILE)
-                n = len(copies)
-                copies.append(
-                    pltpu.make_async_copy(values.at[:, MID + d, rows], stage.at[x, zp, :, j], sems.at[n])
-                )
-    for copy in copies:
-        copy.start()
-    for copy in copies:
-        copy.wait()
+                targets.append((d, stage.at[x, zp, j * ROWS_HERE : (j + 1) * ROWS_HERE]))
+        for d, target in targets:
+            copies.append(pltpu.make_async_copy(values.at[:, MID + d, rows], target, sems.at[len(copies)]))
+    for copy in copies:
+        copy.start()
+    for copy in copies:
+        copy.wait()
+    for x in range(X):
+        for m in range(ROWS_HERE // 2):
+            one, two = diagonal[x, 2 * m], diagonal[x, 2 * m + 1]
+            stage[x, 0, FULL + m] = joined(one, turned(two))
+            stage[x, 1, FULL + m] = joined(turned(one), two)
     copies = [pltpu.make_async_copy(stage, out.at[:, zl], out_sems.at[zl]) for zl in range(ZL)]
     for copy in copies:
         copy.start()
@@ -78,7 +84,7 @@
 
 
 def pack(values):
-    shape = (X, ZP, ROWS_HERE, DEPTH, TILE, BLK)
+    shape = (X, ZP, MESSAGE, TILE, BLK)
     return pl.pallas_call(
         pack_kernel,
         out_shape=pltpu.VMEM((X, ZL) + shape[1:], jnp.bfloat16),
@@ -86,7 +92,8 @@
         out_specs=VMEM,
         scratch_shapes=[
             pltpu.VMEM(shape, jnp.bfloat16),
-            pltpu.SemaphoreType.DMA((X * ZP * DEPTH,)),
+            pltpu.VMEM((X, ROWS_HERE, TILE, BLK), jnp.bfloat16),
+            pltpu.SemaphoreType.DMA((X * (1 + ZP * DEPTH),)),
             pltpu.SemaphoreType.DMA((ZL,)),
         ],
         compiler_params=pltpu.CompilerParams(vmem_limit_bytes=4 * MIB),
@@ -94,27 +101,33 @@
     )(pltpu.with_memory_space_constraint(values, pltpu.HBM))
 
 
-def select_kernel(lists, here, there, out, held, sems):
+def select_kernel(lists, here, there, out, held, halves, sems):
     zl, zp, core = (lax.axis_index(a) for a in ("zl", "zp", "core"))
-    copies = [
-        pltpu.make_async_copy(here, held.at[:, core], sems.at[0]),
-        pltpu.make_async_copy(there, held.at[:, 1 - core], sems.at[1]),
-    ]
-    for copy in copies:
-        copy.start()
-    for copy in copies:
-        copy.wait()
-
-    rows = held.reshape(OWNERS * CORE * ROWS_HERE, DEPTH, TILE, BLK)
+    copies = []
+    for source, c in ((here, core), (there, 1 - core)):
+        for part, target in ((source.at[:, :FULL], held.at[:, c]), (source.at[:, FULL:], halves.at[:, c])):
+            copies.append(pltpu.make_async_copy(part, target, sems.at[len(copies)]))
+    for copy in copies:
+        copy.start()
+    for copy in copies:
+        copy.wait()
+    rows = held.reshape(OWNERS * CORE * FULL, TILE, BLK)
+    pairs = halves.reshape(OWNERS * CORE * ROWS_HERE // 2, TILE, BLK)
 
     def run(cls):
         def one(t, carry):
             owner = ((t // (ZP * Y)) * Z + 2 * zl + lax.rem(t // Y, ZP)) * CORE + core
             row = ROWS_HERE * owner + lax.rem(t, Y)
-            for a, parts in runs(cls):
-                k = jnp.maximum(lists[a, row], 0)
-                for j, length, place in parts:
-                    out[t, place : place + length] = rows[k, j : j + length]
+            target = {a: jnp.maximum(lists[a, row], 0) for a in DIAGONAL}
+            first = {a: k + (k // ROWS_HERE) * (FULL - ROWS_HERE) for a, k in target.items()}
+            for place, (a, s) in enumerate(WANTED[cls]):
+                out[t, place] = rows[first[a] + ROWS_HERE * CLASSES[cls].index(s - a)]
+            for p in range(len(DIAGONAL) // 2):
+                k1, k2 = target[DIAGONAL[2 * p]], target[DIAGONAL[2 * p + 1]]
+                one_half, two_half = pairs[k1 // 2], pairs[k2 // 2]
+                left = jnp.where(lax.rem(k1, 2) == 1, turned(one_half), one_half)
+                right = jnp.where(lax.rem(k2, 2) == 1, two_half, turned(two_half))
+                out[t, BASE + p] = joined(left, right)
             return carry
 
         lax.fori_loop(0, DESTS, one, 0)
@@ -130,8 +143,9 @@
         in_specs=[SMEM, VMEM, VMEM],
         out_specs=VMEM,
         scratch_shapes=[
-            pltpu.VMEM((OWNERS, CORE, ROWS_HERE, DEPTH, TILE, BLK), jnp.bfloat16),
-            pltpu.SemaphoreType.DMA((2,)),
+            pltpu.VMEM((OWNERS, CORE, FULL, TILE, BLK), jnp.bfloat16),
+            pltpu.VMEM((OWNERS, CORE, ROWS_HERE // 2, TILE, BLK), jnp.bfloat16),
+            pltpu.SemaphoreType.DMA((2 * CORE,)),
         ],
         compiler_params=pltpu.CompilerParams(vmem_limit_bytes=12 * MIB),
         name="select",
@@ -184,8 +198,12 @@
         for place, (a, s) in enumerate(WANTED[cls]):
             value = u[cls, place].reshape(BLK, BLK)
             w[blk(a), blk(s)] = value
-            if a != s:
-                w[blk(s), blk(a)] = value.T
+            w[blk(s), blk(a)] = value.T
+    for p in range(len(DIAGONAL) // 2):
+        left, right = (u[cls, BASE + p].reshape(BLK, BLK) for cls in range(ZP))
+        a, s = DIAGONAL[2 * p], DIAGONAL[2 * p + 1]
+        w[blk(a), blk(a)] = joined(left, turned(right))
+        w[blk(s), blk(s)] = joined(turned(left), right)
 
     def mask(value, s):
         return jnp.where(lists[s, row] >= 0, value, jnp.zeros_like(value))
@@ -227,7 +245,7 @@
 
 def body(column_lists, block_values):
     lists = column_lists.T
-    mine = pack(block_values).reshape(OWNERS, ROWS_HERE, DEPTH, TILE, BLK)
+    mine = pack(block_values).reshape(OWNERS, MESSAGE, TILE, BLK)
     here = lax.all_to_all(mine, ("x", "zl", "zp"), 0, 0, tiled=True)
     there = lax.ppermute(here, "core", [(0, 1), (1, 0)])
     asked = select(lists, here, there)

time: 93.8 us -> 94.6 us (level)
  Pallas kernels: 7.33 us -> 10.9 us
  blocking collectives: 82.7 us -> 80.2 us
    pallas_call x1, Pallas kernels: 2.25 us -> 5.54 us  [select(): pl.pallas_call(select_kernel, out_shape=pltpu.VMEM((DESTS, COUNT, TILE, B...]
    all_to_all x1, blocking collectives: 39.8 us -> 37.2 us  [body(): here = lax.all_to_all(mine, ('x', 'zl', 'zp'), 0, 0, tiled=True)]
where the time goes in v4:
time: 94.6 us; the launch traced here: 94.3 us
  blocking collectives  80.2 us (85%)
  Pallas kernels  10.9 us (12%)
  waiting for transfers between devices  2.47 us (3%)
    all_to_all x1, blocking collectives, body(): here = lax.all_to_all(mine, ('x', 'zl', 'zp'), 0, 0, tiled=True)  37.2 us
    all_to_all x1, blocking collectives, body(): got = lax.all_to_all(asked, ('x', 'zp', 'y'), 0, 0, tiled=True)  32.8 us
    all_to_all x1, blocking collectives, body(): mixed = lax.all_to_all(strips, 'y', 0, 0, tiled=True)  10.2 us
    pallas_call x1, Pallas kernels, select(): pl.pallas_call(select_kernel, out_shape=pltpu.VMEM((DESTS, COUNT, TILE, B...  5.54 us
    pallas_call x1, Pallas kernels, purify(): pl.pallas_call(purify_kernel, out_shape=pltpu.VMEM((Y, SLOTS, BLK // Y, B...  3.8 us
    ppermute x1, waiting for transfers between devices, body(): there = lax.ppermute(here, 'core', [(0, 1), (1, 0)])  2.47 us
  transfers between devices with their start and end apart: 1, of which 1 were waited for; matrix products, arithmetic and copies ran while one was open for 0% of the time, Pallas kernels for 0%

profile of v4, /device:TPU:8, one launch (start us, length us, event | category | flops | bytes accessed | tf_op | source)
XLA Modules:
  0.0 94.3 jit_solution(6240004977831602658)
XLA Ops:
  0.0 0.0 copy-start.1
  0.0 1.6 %pack.1 = bf16[4,4,2,14,8,128]{5,4,3,2,1,0:T(8,128)(2,1)S(1)} custom-call(bf16[4,13,128,128]{3,2,1,0:T(8,128)(2,1)} %own.1), custom_call_target="tpu_custom_call" | custom-call | tf_op jit(solution)/shard_map/pack/pallas_call | solution.py:88
  1.6 37.2 %all_to_all.15.here = bf16[32,14,8,128]{3,2,1,0:T(8,128)(2,1)S(1)} all-to-all(bf16[32,14,8,128]{3,2,1,0:T(8,128)(2,1)S(1)} %bitcast.3), channel_id=1, replica_groups=mesh['x'=4,'zl'=4,'zp'=2,'core'=2,'y'=4] {'x','zl','zp'}, dimensions={0} | all-to-all | bytes 1835008 | tf_op jit(solution)/shard_map/all_to_all | solution.py:249
  38.7 0.0 collective-permute-start
  38.7 2.5 %collective-permute-done.there = bf16[32,14,8,128]{3,2,1,0:T(8,128)(2,1)S(1)} collective-permute-done((bf16[32,14,8,128]{3,2,1,0:T(8,128)(2,1)S(1)}, bf16[32,14,8,128]{3,2,1,0:T(8,128)(2,1)S(1)}, u32[]{:S(2)}, u32[]{:S(2)}) %collective-permute-start) | collective-permute-done | bytes 917536 | tf_op jit(solution)/shard_map/ppermute | solution.py:250
  41.2 0.0 copy-done.1
  41.2 5.5 %select.1 = bf16[32,29,8,128]{3,2,1,0:T(8,128)(2,1)S(1)} custom-call(s32[13,256]{1,0:T(8,128)S(1)} %bitcast.4, bf16[32,14,8,128]{3,2,1,0:T(8,128)(2,1)S(1)} %all_to_all.15.here, bf16[32,14,8,128]{3,2,1,0:T(8,128)(2,1)S(1)} %collective-permute-done.there), custom_call_target="tpu_custom_call" | custom-call | tf_op jit(solution)/shard_map/select/pallas_call | solution.py:140
  46.8 0.0 copy-start
  46.8 32.8 %all_to_all.16.got = bf16[32,29,8,128]{3,2,1,0:T(8,128)(2,1)S(1)} all-to-all(bf16[32,29,8,128]{3,2,1,0:T(8,128)(2,1)S(1)} %select.1), channel_id=1, replica_groups=mesh['x'=4,'zl'=4,'zp'=2,'core'=2,'y'=4] {'x','zp','y'}, dimensions={0} | all-to-all | bytes 3801088 | tf_op jit(solution)/shard_map/all_to_all | solution.py:252
  79.6 0.0 copy-done
  79.6 3.8 %purify.1 = bf16[4,13,32,128]{3,2,1,0:T(8,128)(2,1)S(1)} custom-call(s32[13,256]{1,0:T(8,128)S(1)} %bitcast.5, bf16[32,29,8,128]{3,2,1,0:T(8,128)(2,1)S(1)} %all_to_all.16.got, bf16[4,13,128,128]{3,2,1,0:T(8,128)(2,1)S(1)} %copy-done), custom_call_target="tpu_custom_call" | custom-call | tf_op jit(solution)/shard_map/purify/pallas_call | solution.py:230
  83.4 10.2 %all_to_all.17 = bf16[4,13,32,128]{3,2,1,0:T(8,128)(2,1)S(1)} all-to-all(bf16[4,13,32,128]{3,2,1,0:T(8,128)(2,1)S(1)} %purify.1), channel_id=1, replica_groups=mesh['x'=4,'zl'=4,'zp'=2,'core'=2,'y'=4] {'y'}, dimensions={0} | all-to-all | bytes 851968 | tf_op jit(solution)/shard_map/all_to_all | solution.py:254
  93.6 0.8 copy.4
Async XLA Ops:
  0.0 41.2 %copy-start.1 = (s32[256,13]{0,1:T(8,128)S(1)}, s32[256,13]{0,1:T(8,128)}, u32[]{:S(2)}) copy-start(s32[256,13]{0,1:T(8,128)} %param.2) | copy-start | bytes 39940
  38.7 2.5 %collective-permute-start = (bf16[32,14,8,128]{3,2,1,0:T(8,128)(2,1)S(1)}, bf16[32,14,8,128]{3,2,1,0:T(8,128)(2,1)S(1)}, u32[]{:S(2)}, u32[]{:S(2)}) collective-permute-start(bf16[32,14,8,128]{3,2,1,0:T(8,128)(2,1)S(1)} %all_to_all.15.here), channel_id=1, source_target_pairs={{0,4},{4,0},{1,5},{5,1},{2,6},{6,2},{3,7},{7,3},{8,12},{12,8},{9,1... | collective-permute-start | bytes 2752520 | tf_op jit(solution)/shard_map/ppermute | solution.py:250
  46.8 32.8 %copy-start = (bf16[4,13,128,128]{3,2,1,0:T(8,128)(2,1)S(1)}, bf16[4,13,128,128]{3,2,1,0:T(8,128)(2,1)}, u32[]{:S(2)}) copy-start(bf16[4,13,128,128]{3,2,1,0:T(8,128)(2,1)} %own.1) | copy-start | bytes 5111812

commit v5 on v4

--- a/solution.py
+++ b/solution.py
@@ -35,6 +35,7 @@
 BASE = max(len(w) for w in WANTED)
 COUNT = BASE + len(DIAGONAL) // 2
 LANES = BLK // 2
+PAIRS = OWNERS * CORE * ROWS_HERE // 2
 
 
 def turned(value):
@@ -101,32 +102,36 @@
     )(pltpu.with_memory_space_constraint(values, pltpu.HBM))
 
 
-def select_kernel(lists, here, there, out, held, halves, sems):
+def select_kernel(lists, here, there, out, held, came, halves, sems):
     zl, zp, core = (lax.axis_index(a) for a in ("zl", "zp", "core"))
     copies = []
     for source, c in ((here, core), (there, 1 - core)):
-        for part, target in ((source.at[:, :FULL], held.at[:, c]), (source.at[:, FULL:], halves.at[:, c])):
-            copies.append(pltpu.make_async_copy(part, target, sems.at[len(copies)]))
-    for copy in copies:
-        copy.start()
-    for copy in copies:
-        copy.wait()
-    rows = held.reshape(OWNERS * CORE * FULL, TILE, BLK)
-    pairs = halves.reshape(OWNERS * CORE * ROWS_HERE // 2, TILE, BLK)
+        for j in range(DEPTH):
+            part = source.at[:, j * ROWS_HERE : (j + 1) * ROWS_HERE]
+            copies.append(pltpu.make_async_copy(part, held.at[j, :, c], sems.at[len(copies)]))
+        copies.append(pltpu.make_async_copy(source.at[:, FULL:], came.at[:, c], sems.at[len(copies)]))
+    for copy in copies:
+        copy.start()
+    for copy in copies:
+        copy.wait()
+    rows = held.reshape(DEPTH, OWNERS * CORE * ROWS_HERE, TILE, BLK)
+    pairs = came.reshape(PAIRS, TILE, BLK)
+    step = 16
+    for n in range(0, PAIRS, step):
+        value = pairs[n : n + step]
+        halves[n : n + step, 0] = value
+        halves[n : n + step, 1] = turned(value.reshape(step * TILE, BLK)).reshape(step, TILE, BLK)
+    half = halves.reshape(2 * PAIRS, TILE, BLK)
 
     def run(cls):
         def one(t, carry):
-            owner = ((t // (ZP * Y)) * Z + 2 * zl + lax.rem(t // Y, ZP)) * CORE + core
-            row = ROWS_HERE * owner + lax.rem(t, Y)
+            owner = (((t >> 3) * Z + 2 * zl + ((t >> 2) & 1)) << 1) + core
+            row = (owner << 2) + (t & 3)
             target = {a: jnp.maximum(lists[a, row], 0) for a in DIAGONAL}
-            first = {a: k + (k // ROWS_HERE) * (FULL - ROWS_HERE) for a, k in target.items()}
             for place, (a, s) in enumerate(WANTED[cls]):
-                out[t, place] = rows[first[a] + ROWS_HERE * CLASSES[cls].index(s - a)]
+                out[t, place] = rows[CLASSES[cls].index(s - a), target[a]]
             for p in range(len(DIAGONAL) // 2):
-                k1, k2 = target[DIAGONAL[2 * p]], target[DIAGONAL[2 * p + 1]]
-                one_half, two_half = pairs[k1 // 2], pairs[k2 // 2]
-                left = jnp.where(lax.rem(k1, 2) == 1, turned(one_half), one_half)
-                right = jnp.where(lax.rem(k2, 2) == 1, two_half, turned(two_half))
+                left, right = half[target[DIAGONAL[2 * p]]], half[target[DIAGONAL[2 * p + 1]] ^ 1]
                 out[t, BASE + p] = joined(left, right)
             return carry
 
@@ -143,9 +148,10 @@
         in_specs=[SMEM, VMEM, VMEM],
         out_specs=VMEM,
         scratch_shapes=[
-            pltpu.VMEM((OWNERS, CORE, FULL, TILE, BLK), jnp.bfloat16),
+            pltpu.VMEM((DEPTH, OWNERS, CORE, ROWS_HERE, TILE, BLK), jnp.bfloat16),
             pltpu.VMEM((OWNERS, CORE, ROWS_HERE // 2, TILE, BLK), jnp.bfloat16),
-            pltpu.SemaphoreType.DMA((2 * CORE,)),
+            pltpu.VMEM((PAIRS, 2, TILE, BLK), jnp.bfloat16),
+            pltpu.SemaphoreType.DMA((CORE * (DEPTH + 1),)),
         ],
         compiler_params=pltpu.CompilerParams(vmem_limit_bytes=12 * MIB),
         name="select",

time: 94.6 us -> 91.3 us (0.965)
  Pallas kernels: 10.9 us -> 7.79 us
    pallas_call x1, Pallas kernels: 5.54 us -> 2.43 us  [select(): pl.pallas_call(select_kernel, out_shape=pltpu.VMEM((DESTS, COUNT, TILE, B...]
where the time goes in v5:
time: 91.3 us; the launch traced here: 91.1 us
  blocking collectives  80 us (88%)
  Pallas kernels  7.79 us (9%)
  waiting for transfers between devices  2.47 us (3%)
    all_to_all x1, blocking collectives, body(): here = lax.all_to_all(mine, ('x', 'zl', 'zp'), 0, 0, tiled=True)  37.2 us
    all_to_all x1, blocking collectives, body(): got = lax.all_to_all(asked, ('x', 'zp', 'y'), 0, 0, tiled=True)  32.7 us
    all_to_all x1, blocking collectives, body(): mixed = lax.all_to_all(strips, 'y', 0, 0, tiled=True)  10.1 us
    pallas_call x1, Pallas kernels, purify(): pl.pallas_call(purify_kernel, out_shape=pltpu.VMEM((Y, SLOTS, BLK // Y, B...  3.8 us
    ppermute x1, waiting for transfers between devices, body(): there = lax.ppermute(here, 'core', [(0, 1), (1, 0)])  2.47 us
    pallas_call x1, Pallas kernels, select(): pl.pallas_call(select_kernel, out_shape=pltpu.VMEM((DESTS, COUNT, TILE, B...  2.43 us
  transfers between devices with their start and end apart: 1, of which 1 were waited for; matrix products, arithmetic and copies ran while one was open for 0% of the time, Pallas kernels for 0%

profile of v5, /device:TPU:8, one launch (start us, length us, event | category | flops | bytes accessed | tf_op | source)
XLA Modules:
  0.0 91.1 jit_solution(14369700181559401051)
XLA Ops:
  0.0 0.0 copy-start.1
  0.0 1.6 %pack.1 = bf16[4,4,2,14,8,128]{5,4,3,2,1,0:T(8,128)(2,1)S(1)} custom-call(bf16[4,13,128,128]{3,2,1,0:T(8,128)(2,1)} %own.1), custom_call_target="tpu_custom_call" | custom-call | tf_op jit(solution)/shard_map/pack/pallas_call | solution.py:89
  1.6 37.2 %all_to_all.15.here = bf16[32,14,8,128]{3,2,1,0:T(8,128)(2,1)S(1)} all-to-all(bf16[32,14,8,128]{3,2,1,0:T(8,128)(2,1)S(1)} %bitcast.3), channel_id=1, replica_groups=mesh['x'=4,'zl'=4,'zp'=2,'core'=2,'y'=4] {'x','zl','zp'}, dimensions={0} | all-to-all | bytes 1835008 | tf_op jit(solution)/shard_map/all_to_all | solution.py:255
  38.7 0.0 collective-permute-start
  38.7 2.5 %collective-permute-done.there = bf16[32,14,8,128]{3,2,1,0:T(8,128)(2,1)S(1)} collective-permute-done((bf16[32,14,8,128]{3,2,1,0:T(8,128)(2,1)S(1)}, bf16[32,14,8,128]{3,2,1,0:T(8,128)(2,1)S(1)}, u32[]{:S(2)}, u32[]{:S(2)}) %collective-permute-start) | collective-permute-done | bytes 917536 | tf_op jit(solution)/shard_map/ppermute | solution.py:256
  41.2 0.0 copy-done.1
  41.2 2.4 %select.1 = bf16[32,29,8,128]{3,2,1,0:T(8,128)(2,1)S(1)} custom-call(s32[13,256]{1,0:T(8,128)S(1)} %bitcast.4, bf16[32,14,8,128]{3,2,1,0:T(8,128)(2,1)S(1)} %all_to_all.15.here, bf16[32,14,8,128]{3,2,1,0:T(8,128)(2,1)S(1)} %collective-permute-done.there), custom_call_target="tpu_custom_call" | custom-call | tf_op jit(solution)/shard_map/select/pallas_call | solution.py:145
  43.6 0.0 copy-start
  43.7 32.7 %all_to_all.16.got = bf16[32,29,8,128]{3,2,1,0:T(8,128)(2,1)S(1)} all-to-all(bf16[32,29,8,128]{3,2,1,0:T(8,128)(2,1)S(1)} %select.1), channel_id=1, replica_groups=mesh['x'=4,'zl'=4,'zp'=2,'core'=2,'y'=4] {'x','zp','y'}, dimensions={0} | all-to-all | bytes 3801088 | tf_op jit(solution)/shard_map/all_to_all | solution.py:258
  76.4 0.0 copy-done
  76.4 3.8 %purify.1 = bf16[4,13,32,128]{3,2,1,0:T(8,128)(2,1)S(1)} custom-call(s32[13,256]{1,0:T(8,128)S(1)} %bitcast.5, bf16[32,29,8,128]{3,2,1,0:T(8,128)(2,1)S(1)} %all_to_all.16.got, bf16[4,13,128,128]{3,2,1,0:T(8,128)(2,1)S(1)} %copy-done), custom_call_target="tpu_custom_call" | custom-call | tf_op jit(solution)/shard_map/purify/pallas_call | solution.py:236
  80.2 10.1 %all_to_all.17 = bf16[4,13,32,128]{3,2,1,0:T(8,128)(2,1)S(1)} all-to-all(bf16[4,13,32,128]{3,2,1,0:T(8,128)(2,1)S(1)} %purify.1), channel_id=1, replica_groups=mesh['x'=4,'zl'=4,'zp'=2,'core'=2,'y'=4] {'y'}, dimensions={0} | all-to-all | bytes 851968 | tf_op jit(solution)/shard_map/all_to_all | solution.py:260
  90.3 0.8 copy.4
Async XLA Ops:
  0.0 41.2 %copy-start.1 = (s32[256,13]{0,1:T(8,128)S(1)}, s32[256,13]{0,1:T(8,128)}, u32[]{:S(2)}) copy-start(s32[256,13]{0,1:T(8,128)} %param.2) | copy-start | bytes 39940
  38.7 2.5 %collective-permute-start = (bf16[32,14,8,128]{3,2,1,0:T(8,128)(2,1)S(1)}, bf16[32,14,8,128]{3,2,1,0:T(8,128)(2,1)S(1)}, u32[]{:S(2)}, u32[]{:S(2)}) collective-permute-start(bf16[32,14,8,128]{3,2,1,0:T(8,128)(2,1)S(1)} %all_to_all.15.here), channel_id=1, source_target_pairs={{0,4},{4,0},{1,5},{5,1},{2,6},{6,2},{3,7},{7,3},{8,12},{12,8},{9,1... | collective-permute-start | bytes 2752520 | tf_op jit(solution)/shard_map/ppermute | solution.py:256
  43.6 32.7 %copy-start = (bf16[4,13,128,128]{3,2,1,0:T(8,128)(2,1)S(1)}, bf16[4,13,128,128]{3,2,1,0:T(8,128)(2,1)}, u32[]{:S(2)}) copy-start(bf16[4,13,128,128]{3,2,1,0:T(8,128)(2,1)} %own.1) | copy-start | bytes 5111812

commit v6 on v5

--- a/solution.py
+++ b/solution.py
@@ -171,42 +171,32 @@
 GROUPS = groups()
 
 
-def purify_kernel(lists, got, own, out, u, w, sq, sems):
+def purify_kernel(lists, got, own, out, w, sq):
     x, zl, zp, core, y = (lax.axis_index(a) for a in AXES)
     row = ROWS_HERE * ((x * Z + 2 * zl + zp) * CORE + core) + y
-    copies = []
-    for p in range(DESTS):
-        tile = (p // (ZP * Y)) * Y + p % Y
-        copies.append(pltpu.make_async_copy(got.at[p], u.at[(p // Y) % ZP, :, tile], sems.at[p]))
-    for s in range(SLOTS):
-        copies.append(
-            pltpu.make_async_copy(
-                own.at[y, s],
-                w.at[MID * BLK : (MID + 1) * BLK, s * BLK : (s + 1) * BLK],
-                sems.at[DESTS + s],
-            )
-        )
-    for copy in copies:
-        copy.start()
 
     def blk(a):
         return slice(a * BLK, (a + 1) * BLK)
+
+    def sent(cls, place):
+        tiles = [got[((t // Y) * ZP + cls) * Y + t % Y, place] for t in range(TILES)]
+        return jnp.concatenate(tiles, axis=0)
 
     for a in range(SLOTS - HALF):
         w[blk(a), blk(a + HALF)] = jnp.zeros((BLK, BLK), jnp.bfloat16)
         w[blk(a + HALF), blk(a)] = jnp.zeros((BLK, BLK), jnp.bfloat16)
-    for copy in copies:
-        copy.wait()
     for s in range(SLOTS):
+        value = own[y, s]
+        w[blk(MID), blk(s)] = value
         if s != MID:
-            w[blk(s), blk(MID)] = w[blk(MID), blk(s)].T
+            w[blk(s), blk(MID)] = value.T
     for cls in range(ZP):
         for place, (a, s) in enumerate(WANTED[cls]):
-            value = u[cls, place].reshape(BLK, BLK)
+            value = sent(cls, place)
             w[blk(a), blk(s)] = value
             w[blk(s), blk(a)] = value.T
     for p in range(len(DIAGONAL) // 2):
-        left, right = (u[cls, BASE + p].reshape(BLK, BLK) for cls in range(ZP))
+        left, right = (sent(cls, BASE + p) for cls in range(ZP))
         a, s = DIAGONAL[2 * p], DIAGONAL[2 * p + 1]
         w[blk(a), blk(a)] = joined(left, turned(right))
         w[blk(s), blk(s)] = joined(turned(left), right)
@@ -236,17 +226,15 @@
     return pl.pallas_call(
         purify_kernel,
         out_shape=pltpu.VMEM((Y, SLOTS, BLK // Y, BLK), jnp.bfloat16),
-        in_specs=[SMEM, VMEM, ANY],
+        in_specs=[SMEM, VMEM, VMEM],
         out_specs=VMEM,
         scratch_shapes=[
-            pltpu.VMEM((ZP, COUNT, TILES, TILE, BLK), jnp.bfloat16),
             pltpu.VMEM((SLOTS * BLK, SLOTS * BLK), jnp.bfloat16),
             pltpu.VMEM((BLK, SLOTS * BLK), jnp.bfloat16),
-            pltpu.SemaphoreType.DMA((DESTS + SLOTS,)),
         ],
         compiler_params=pltpu.CompilerParams(vmem_limit_bytes=24 * MIB),
         name="purify",
-    )(lists, near(got), own)
+    )(lists, near(got), near(own))
 
 
 def body(column_lists, block_values):

time: 91.3 us -> 90.3 us (0.989)
  Pallas kernels: 7.79 us -> 6.7 us
    pallas_call x1, Pallas kernels: 3.8 us -> 2.72 us  [purify(): pl.pallas_call(purify_kernel, out_shape=pltpu.VMEM((Y, SLOTS, BLK // Y, B...]
where the time goes in v6:
time: 90.3 us; the launch traced here: 90 us
  blocking collectives  80 us (89%)
  Pallas kernels  6.7 us (7%)
  waiting for transfers between devices  2.47 us (3%)
    all_to_all x1, blocking collectives, body(): here = lax.all_to_all(mine, ('x', 'zl', 'zp'), 0, 0, tiled=True)  37.2 us
    all_to_all x1, blocking collectives, body(): got = lax.all_to_all(asked, ('x', 'zp', 'y'), 0, 0, tiled=True)  32.7 us
    all_to_all x1, blocking collectives, body(): mixed = lax.all_to_all(strips, 'y', 0, 0, tiled=True)  10.1 us
    pallas_call x1, Pallas kernels, purify(): pl.pallas_call(purify_kernel, out_shape=pltpu.VMEM((Y, SLOTS, BLK // Y, B...  2.72 us
    ppermute x1, waiting for transfers between devices, body(): there = lax.ppermute(here, 'core', [(0, 1), (1, 0)])  2.47 us
    pallas_call x1, Pallas kernels, select(): pl.pallas_call(select_kernel, out_shape=pltpu.VMEM((DESTS, COUNT, TILE, B...  2.43 us
  transfers between devices with their start and end apart: 1, of which 1 were waited for; matrix products, arithmetic and copies ran while one was open for 0% of the time, Pallas kernels for 0%

profile of v6, /device:TPU:8, one launch (start us, length us, event | category | flops | bytes accessed | tf_op | source)
XLA Modules:
  0.0 90.0 jit_solution(11232976733862195732)
XLA Ops:
  0.0 0.0 copy-start.1
  0.0 1.6 %pack.1 = bf16[4,4,2,14,8,128]{5,4,3,2,1,0:T(8,128)(2,1)S(1)} custom-call(bf16[4,13,128,128]{3,2,1,0:T(8,128)(2,1)} %own.1), custom_call_target="tpu_custom_call" | custom-call | tf_op jit(solution)/shard_map/pack/pallas_call | solution.py:89
  1.6 37.2 %all_to_all.15.here = bf16[32,14,8,128]{3,2,1,0:T(8,128)(2,1)S(1)} all-to-all(bf16[32,14,8,128]{3,2,1,0:T(8,128)(2,1)S(1)} %bitcast.3), channel_id=1, replica_groups=mesh['x'=4,'zl'=4,'zp'=2,'core'=2,'y'=4] {'x','zl','zp'}, dimensions={0} | all-to-all | bytes 1835008 | tf_op jit(solution)/shard_map/all_to_all | solution.py:243
  38.7 0.0 collective-permute-start
  38.7 2.5 %collective-permute-done.there = bf16[32,14,8,128]{3,2,1,0:T(8,128)(2,1)S(1)} collective-permute-done((bf16[32,14,8,128]{3,2,1,0:T(8,128)(2,1)S(1)}, bf16[32,14,8,128]{3,2,1,0:T(8,128)(2,1)S(1)}, u32[]{:S(2)}, u32[]{:S(2)}) %collective-permute-start) | collective-permute-done | bytes 917536 | tf_op jit(solution)/shard_map/ppermute | solution.py:244
  41.2 0.0 copy-done.1
  41.2 2.4 %select.1 = bf16[32,29,8,128]{3,2,1,0:T(8,128)(2,1)S(1)} custom-call(s32[13,256]{1,0:T(8,128)S(1)} %bitcast.4, bf16[32,14,8,128]{3,2,1,0:T(8,128)(2,1)S(1)} %all_to_all.15.here, bf16[32,14,8,128]{3,2,1,0:T(8,128)(2,1)S(1)} %collective-permute-done.there), custom_call_target="tpu_custom_call" | custom-call | tf_op jit(solution)/shard_map/select/pallas_call | solution.py:145
  43.6 0.0 copy-start
  43.7 32.7 %all_to_all.16.got = bf16[32,29,8,128]{3,2,1,0:T(8,128)(2,1)S(1)} all-to-all(bf16[32,29,8,128]{3,2,1,0:T(8,128)(2,1)S(1)} %select.1), channel_id=1, replica_groups=mesh['x'=4,'zl'=4,'zp'=2,'core'=2,'y'=4] {'x','zp','y'}, dimensions={0} | all-to-all | bytes 3801088 | tf_op jit(solution)/shard_map/all_to_all | solution.py:246
  76.4 0.0 copy-done
  76.4 2.7 %purify.1 = bf16[4,13,32,128]{3,2,1,0:T(8,128)(2,1)S(1)} custom-call(s32[13,256]{1,0:T(8,128)S(1)} %bitcast.5, bf16[32,29,8,128]{3,2,1,0:T(8,128)(2,1)S(1)} %all_to_all.16.got, bf16[4,13,128,128]{3,2,1,0:T(8,128)(2,1)S(1)} %copy-done), custom_call_target="tpu_custom_call" | custom-call | tf_op jit(solution)/shard_map/purify/pallas_call | solution.py:226
  79.1 10.1 %all_to_all.17 = bf16[4,13,32,128]{3,2,1,0:T(8,128)(2,1)S(1)} all-to-all(bf16[4,13,32,128]{3,2,1,0:T(8,128)(2,1)S(1)} %purify.1), channel_id=1, replica_groups=mesh['x'=4,'zl'=4,'zp'=2,'core'=2,'y'=4] {'y'}, dimensions={0} | all-to-all | bytes 851968 | tf_op jit(solution)/shard_map/all_to_all | solution.py:248
  89.2 0.8 copy.4
Async XLA Ops:
  0.0 41.2 %copy-start.1 = (s32[256,13]{0,1:T(8,128)S(1)}, s32[256,13]{0,1:T(8,128)}, u32[]{:S(2)}) copy-start(s32[256,13]{0,1:T(8,128)} %param.2) | copy-start | bytes 39940
  38.7 2.5 %collective-permute-start = (bf16[32,14,8,128]{3,2,1,0:T(8,128)(2,1)S(1)}, bf16[32,14,8,128]{3,2,1,0:T(8,128)(2,1)S(1)}, u32[]{:S(2)}, u32[]{:S(2)}) collective-permute-start(bf16[32,14,8,128]{3,2,1,0:T(8,128)(2,1)S(1)} %all_to_all.15.here), channel_id=1, source_target_pairs={{0,4},{4,0},{1,5},{5,1},{2,6},{6,2},{3,7},{7,3},{8,12},{12,8},{9,1... | collective-permute-start | bytes 2752520 | tf_op jit(solution)/shard_map/ppermute | solution.py:244
  43.6 32.7 %copy-start = (bf16[4,13,128,128]{3,2,1,0:T(8,128)(2,1)S(1)}, bf16[4,13,128,128]{3,2,1,0:T(8,128)(2,1)}, u32[]{:S(2)}) copy-start(bf16[4,13,128,128]{3,2,1,0:T(8,128)(2,1)} %own.1) | copy-start | bytes 5111812

commit v7 on v6

--- a/solution.py
+++ b/solution.py
@@ -219,7 +219,7 @@
             value = 3.0 * sq[:, blk(s + j)].astype(jnp.float32) - 2.0 * total[:, blk(j)]
             value = mask(value, s + j).T.astype(jnp.bfloat16)
             for part in range(Y):
-                out[part, s + j] = value[part * (BLK // Y) : (part + 1) * (BLK // Y)]
+                out[(part - y) & (Y - 1), s + j] = value[part * (BLK // Y) : (part + 1) * (BLK // Y)]
 
 
 def purify(lists, got, own):
@@ -237,6 +237,28 @@
     )(lists, near(got), near(own))
 
 
+def place_kernel(own, one, two, three, out, sems):
+    y = lax.axis_index("y")
+    parts = (own.at[0], one, two, three)
+    copies = [pltpu.make_async_copy(part, out.at[(y - n) & (Y - 1)], sems.at[n]) for n, part in enumerate(parts)]
+    for copy in copies:
+        copy.start()
+    for copy in copies:
+        copy.wait()
+
+
+def place(strips, parts):
+    return pl.pallas_call(
+        place_kernel,
+        out_shape=pltpu.HBM((Y, SLOTS, BLK // Y, BLK), jnp.bfloat16),
+        in_specs=[VMEM] * Y,
+        out_specs=pl.BlockSpec(memory_space=pltpu.HBM),
+        scratch_shapes=[pltpu.SemaphoreType.DMA((Y,))],
+        compiler_params=pltpu.CompilerParams(vmem_limit_bytes=4 * MIB),
+        name="place",
+    )(*(near(p) for p in (strips, *parts)))
+
+
 def body(column_lists, block_values):
     lists = column_lists.T
     mine = pack(block_values).reshape(OWNERS, MESSAGE, TILE, BLK)
@@ -245,7 +267,10 @@
     asked = select(lists, here, there)
     got = lax.all_to_all(asked, ("x", "zp", "y"), 0, 0, tiled=True)
     strips = purify(lists, got, block_values)
-    mixed = lax.all_to_all(strips, "y", 0, 0, tiled=True)
+    two, one, three = (
+        lax.ppermute(strips[n], "y", [(i, (i + n) % Y) for i in range(Y)]) for n in (2, 1, 3)
+    )
+    mixed = place(strips, (one, two, three))
     return mixed.transpose(0, 1, 3, 2)
 
 

time: 90.3 us -> 88.9 us (0.984)
  blocking collectives: 80 us -> 69.9 us
  waiting for transfers between devices: 2.47 us -> 7.23 us
  starting transfers between devices: 0.01 us -> 3.28 us
    all_to_all x1 -> x0, blocking collectives: 10.1 us -> none  [body(): mixed = lax.all_to_all(strips, 'y', 0, 0, tiled=True)]
    ppermute x0 -> x3, waiting for transfers between devices: none -> 4.76 us  [body(): lax.ppermute(strips[n], 'y', [(i, (i + n) % Y) for i in range(Y)])]
    ppermute x0 -> x3, starting transfers between devices: none -> 3.27 us  [body(): lax.ppermute(strips[n], 'y', [(i, (i + n) % Y) for i in range(Y)])]
  transfers between devices with their start and end apart: 1 -> 4, of which waited for: 1 -> 4; matrix products, arithmetic and copies ran while one was open for 0% -> 0% of each run, Pallas kernels for 0% -> 0%
where the time goes in v7:
time: 88.9 us; the launch traced here: 88 us
  blocking collectives  69.9 us (79%)
  Pallas kernels  7.49 us (8%)
  waiting for transfers between devices  7.23 us (8%)
  starting transfers between devices  3.28 us (4%)
    all_to_all x1, blocking collectives, body(): here = lax.all_to_all(mine, ('x', 'zl', 'zp'), 0, 0, tiled=True)  37.2 us
    all_to_all x1, blocking collectives, body(): got = lax.all_to_all(asked, ('x', 'zp', 'y'), 0, 0, tiled=True)  32.7 us
    ppermute x3, waiting for transfers between devices, body(): lax.ppermute(strips[n], 'y', [(i, (i + n) % Y) for i in range(Y)])  4.76 us
    ppermute x3, starting transfers between devices, body(): lax.ppermute(strips[n], 'y', [(i, (i + n) % Y) for i in range(Y)])  3.27 us
    pallas_call x1, Pallas kernels, purify(): pl.pallas_call(purify_kernel, out_shape=pltpu.VMEM((Y, SLOTS, BLK // Y, B...  2.72 us
    ppermute x1, waiting for transfers between devices, body(): there = lax.ppermute(here, 'core', [(0, 1), (1, 0)])  2.47 us
    pallas_call x1, Pallas kernels, select(): pl.pallas_call(select_kernel, out_shape=pltpu.VMEM((DESTS, COUNT, TILE, B...  2.43 us
  transfers between devices with their start and end apart: 4, of which 4 were waited for; matrix products, arithmetic and copies ran while one was open for 0% of the time, Pallas kernels for 0%

profile of v7, /device:TPU:8, one launch (start us, length us, event | category | flops | bytes accessed | tf_op | source)
XLA Modules:
  0.0 88.0 jit_solution(11345639406821587326)
XLA Ops:
  0.0 0.0 copy-start.1
  0.0 1.6 %pack.1 = bf16[4,4,2,14,8,128]{5,4,3,2,1,0:T(8,128)(2,1)S(1)} custom-call(bf16[4,13,128,128]{3,2,1,0:T(8,128)(2,1)} %own.1), custom_call_target="tpu_custom_call" | custom-call | tf_op jit(solution)/shard_map/pack/pallas_call | solution.py:89
  1.6 37.2 %all_to_all.10.here = bf16[32,14,8,128]{3,2,1,0:T(8,128)(2,1)S(1)} all-to-all(bf16[32,14,8,128]{3,2,1,0:T(8,128)(2,1)S(1)} %bitcast.9), channel_id=1, replica_groups=mesh['x'=4,'zl'=4,'zp'=2,'core'=2,'y'=4] {'x','zl','zp'}, dimensions={0} | all-to-all | bytes 1835008 | tf_op jit(solution)/shard_map/all_to_all | solution.py:265
  38.7 0.0 collective-permute-start
  38.7 2.5 %collective-permute-done.there = bf16[32,14,8,128]{3,2,1,0:T(8,128)(2,1)S(1)} collective-permute-done((bf16[32,14,8,128]{3,2,1,0:T(8,128)(2,1)S(1)}, bf16[32,14,8,128]{3,2,1,0:T(8,128)(2,1)S(1)}, u32[]{:S(2)}, u32[]{:S(2)}) %collective-permute-start) | collective-permute-done | bytes 917536 | tf_op jit(solution)/shard_map/ppermute | solution.py:266
  41.2 0.0 copy-done.1
  41.2 2.4 %select.1 = bf16[32,29,8,128]{3,2,1,0:T(8,128)(2,1)S(1)} custom-call(s32[13,256]{1,0:T(8,128)S(1)} %bitcast.10, bf16[32,14,8,128]{3,2,1,0:T(8,128)(2,1)S(1)} %all_to_all.10.here, bf16[32,14,8,128]{3,2,1,0:T(8,128)(2,1)S(1)} %collective-permute-done.there), custom_call_target="tpu_custom_call" | custom-call | tf_op jit(solution)/shard_map/select/pallas_call | solution.py:145
  43.6 0.0 copy-start
  43.7 32.7 %all_to_all.11.got = bf16[32,29,8,128]{3,2,1,0:T(8,128)(2,1)S(1)} all-to-all(bf16[32,29,8,128]{3,2,1,0:T(8,128)(2,1)S(1)} %select.1), channel_id=1, replica_groups=mesh['x'=4,'zl'=4,'zp'=2,'core'=2,'y'=4] {'x','zp','y'}, dimensions={0} | all-to-all | bytes 3801088 | tf_op jit(solution)/shard_map/all_to_all | solution.py:268
  76.4 0.0 copy-done
  76.4 2.7 %purify.1.own = bf16[4,13,32,128]{3,2,1,0:T(8,128)(2,1)S(1)} custom-call(s32[13,256]{1,0:T(8,128)S(1)} %bitcast.11, bf16[32,29,8,128]{3,2,1,0:T(8,128)(2,1)S(1)} %all_to_all.11.got, bf16[4,13,128,128]{3,2,1,0:T(8,128)(2,1)S(1)} %copy-done), custom_call_target="tpu_custom_call" | custom-call | tf_op jit(solution)/shard_map/purify/pallas_call | solution.py:226
  79.1 0.4 collective-permute-start.3
  79.5 2.0 %collective-permute-start.2 = (bf16[13,32,128]{2,1,0:T(8,128)(2,1)S(1)}, bf16[13,32,128]{2,1,0:T(8,128)(2,1)S(1)}, u32[]{:S(2)}, u32[]{:S(2)}) collective-permute-start(bf16[13,32,128]{2,1,0:T(8,128)(2,1)S(1)} %get-tuple-element.6), channel_id=1, source_target_pairs={{0,2},{1,3},{2,0},{3,1},{4,6},{5,7},{6,4},{7,5},{8,10},{9,11},{10,... | collective-permute-start | bytes 319496 | tf_op jit(solution)/shard_map/ppermute | solution.py:271
  81.6 0.8 collective-permute-start.1
  82.4 2.2 %collective-permute-done.3.three = bf16[13,32,128]{2,1,0:T(8,128)(2,1)S(1)} collective-permute-done((bf16[13,32,128]{2,1,0:T(8,128)(2,1)S(1)}, bf16[13,32,128]{2,1,0:T(8,128)(2,1)S(1)}, u32[]{:S(2)}, u32[]{:S(2)}) %collective-permute-start.3) | collective-permute-done | bytes 106528 | tf_op jit(solution)/shard_map/ppermute | solution.py:271
  84.6 1.1 %collective-permute-done.2.two = bf16[13,32,128]{2,1,0:T(8,128)(2,1)S(1)} collective-permute-done((bf16[13,32,128]{2,1,0:T(8,128)(2,1)S(1)}, bf16[13,32,128]{2,1,0:T(8,128)(2,1)S(1)}, u32[]{:S(2)}, u32[]{:S(2)}) %collective-permute-start.2) | collective-permute-done | bytes 106528 | tf_op jit(solution)/shard_map/ppermute | solution.py:271
  85.8 1.4 %collective-permute-done.1.one = bf16[13,32,128]{2,1,0:T(8,128)(2,1)S(1)} collective-permute-done((bf16[13,32,128]{2,1,0:T(8,128)(2,1)S(1)}, bf16[13,32,128]{2,1,0:T(8,128)(2,1)S(1)}, u32[]{:S(2)}, u32[]{:S(2)}) %collective-permute-start.1) | collective-permute-done | bytes 106528 | tf_op jit(solution)/shard_map/ppermute | solution.py:271
  87.2 0.8 place.1
  (1 shorter events, 0.0 us)
Async XLA Ops:
  0.0 41.2 %copy-start.1 = (s32[256,13]{0,1:T(8,128)S(1)}, s32[256,13]{0,1:T(8,128)}, u32[]{:S(2)}) copy-start(s32[256,13]{0,1:T(8,128)} %param.2) | copy-start | bytes 39940
  38.7 2.5 %collective-permute-start = (bf16[32,14,8,128]{3,2,1,0:T(8,128)(2,1)S(1)}, bf16[32,14,8,128]{3,2,1,0:T(8,128)(2,1)S(1)}, u32[]{:S(2)}, u32[]{:S(2)}) collective-permute-start(bf16[32,14,8,128]{3,2,1,0:T(8,128)(2,1)S(1)} %all_to_all.10.here), channel_id=1, source_target_pairs={{0,4},{4,0},{1,5},{5,1},{2,6},{6,2},{3,7},{7,3},{8,12},{12,8},{9,1... | collective-permute-start | bytes 2752520 | tf_op jit(solution)/shard_map/ppermute | solution.py:266
  43.6 32.7 %copy-start = (bf16[4,13,128,128]{3,2,1,0:T(8,128)(2,1)S(1)}, bf16[4,13,128,128]{3,2,1,0:T(8,128)(2,1)}, u32[]{:S(2)}) copy-start(bf16[4,13,128,128]{3,2,1,0:T(8,128)(2,1)} %own.1) | copy-start | bytes 5111812
  79.1 5.5 %collective-permute-start.3 = (bf16[13,32,128]{2,1,0:T(8,128)(2,1)S(1)}, bf16[13,32,128]{2,1,0:T(8,128)(2,1)S(1)}, u32[]{:S(2)}, u32[]{:S(2)}) collective-permute-start(bf16[13,32,128]{2,1,0:T(8,128)(2,1)S(1)} %get-tuple-element.5), channel_id=1, source_target_pairs={{0,3},{1,0},{2,1},{3,2},{4,7},{5,4},{6,5},{7,6},{8,11},{9,8},{10,9... | collective-permute-start | bytes 319496 | tf_op jit(solution)/shard_map/ppermute | solution.py:271
  79.5 6.2 %collective-permute-start.2 = (bf16[13,32,128]{2,1,0:T(8,128)(2,1)S(1)}, bf16[13,32,128]{2,1,0:T(8,128)(2,1)S(1)}, u32[]{:S(2)}, u32[]{:S(2)}) collective-permute-start(bf16[13,32,128]{2,1,0:T(8,128)(2,1)S(1)} %get-tuple-element.6), channel_id=1, source_target_pairs={{0,2},{1,3},{2,0},{3,1},{4,6},{5,7},{6,4},{7,5},{8,10},{9,11},{10,... | collective-permute-start | bytes 319496 | tf_op jit(solution)/shard_map/ppermute | solution.py:271
  81.6 5.6 %collective-permute-start.1 = (bf16[13,32,128]{2,1,0:T(8,128)(2,1)S(1)}, bf16[13,32,128]{2,1,0:T(8,128)(2,1)S(1)}, u32[]{:S(2)}, u32[]{:S(2)}) collective-permute-start(bf16[13,32,128]{2,1,0:T(8,128)(2,1)S(1)} %get-tuple-element.7), channel_id=1, source_target_pairs={{0,1},{1,2},{2,3},{3,0},{4,5},{5,6},{6,7},{7,4},{8,9},{9,10},{10,1... | collective-permute-start | bytes 319496 | tf_op jit(solution)/shard_map/ppermute | solution.py:271

commit v8 on v7

--- a/solution.py
+++ b/solution.py
@@ -35,6 +35,7 @@
 BASE = max(len(w) for w in WANTED)
 COUNT = BASE + len(DIAGONAL) // 2
 LANES = BLK // 2
+PARTS = ((0, slice(0, X)), (1, slice(0, X)), (-1, slice(0, X)), (2, slice(0, X // 2)), (2, slice(X // 2, X)))
 PAIRS = OWNERS * CORE * ROWS_HERE // 2
 
 
@@ -57,7 +58,7 @@
     return pltpu.with_memory_space_constraint(value, pltpu.VMEM)
 
 
-def pack_kernel(values, out, stage, diagonal, sems, out_sems):
+def pack_kernel(values, out, diagonal, sems):
     y = lax.axis_index("y")
     copies = []
     for x in range(X):
@@ -65,7 +66,7 @@
         targets = [(0, diagonal.at[x])]
         for zp in range(ZP):
             for j, d in enumerate(CLASSES[zp]):
-                targets.append((d, stage.at[x, zp, j * ROWS_HERE : (j + 1) * ROWS_HERE]))
+                targets.append((d, out.at[x, zp, j * ROWS_HERE : (j + 1) * ROWS_HERE]))
         for d, target in targets:
             copies.append(pltpu.make_async_copy(values.at[:, MID + d, rows], target, sems.at[len(copies)]))
     for copy in copies:
@@ -75,41 +76,37 @@
     for x in range(X):
         for m in range(ROWS_HERE // 2):
             one, two = diagonal[x, 2 * m], diagonal[x, 2 * m + 1]
-            stage[x, 0, FULL + m] = joined(one, turned(two))
-            stage[x, 1, FULL + m] = joined(turned(one), two)
-    copies = [pltpu.make_async_copy(stage, out.at[:, zl], out_sems.at[zl]) for zl in range(ZL)]
-    for copy in copies:
-        copy.start()
-    for copy in copies:
-        copy.wait()
+            out[x, 0, FULL + m] = joined(one, turned(two))
+            out[x, 1, FULL + m] = joined(turned(one), two)
 
 
 def pack(values):
-    shape = (X, ZP, MESSAGE, TILE, BLK)
     return pl.pallas_call(
         pack_kernel,
-        out_shape=pltpu.VMEM((X, ZL) + shape[1:], jnp.bfloat16),
+        out_shape=pltpu.VMEM((X, ZP, MESSAGE, TILE, BLK), jnp.bfloat16),
         in_specs=[ANY],
         out_specs=VMEM,
         scratch_shapes=[
-            pltpu.VMEM(shape, jnp.bfloat16),
             pltpu.VMEM((X, ROWS_HERE, TILE, BLK), jnp.bfloat16),
             pltpu.SemaphoreType.DMA((X * (1 + ZP * DEPTH),)),
-            pltpu.SemaphoreType.DMA((ZL,)),
         ],
         compiler_params=pltpu.CompilerParams(vmem_limit_bytes=4 * MIB),
         name="pack",
     )(pltpu.with_memory_space_constraint(values, pltpu.HBM))
 
 
-def select_kernel(lists, here, there, out, held, came, halves, sems):
+def select_kernel(lists, *refs):
+    pieces, (out, held, came, halves, sems) = refs[: 2 * len(PARTS)], refs[2 * len(PARTS) :]
     zl, zp, core = (lax.axis_index(a) for a in ("zl", "zp", "core"))
     copies = []
-    for source, c in ((here, core), (there, 1 - core)):
+    for n, source in enumerate(pieces):
+        c = core if n < len(PARTS) else 1 - core
+        step, xs = PARTS[n % len(PARTS)]
+        there = (zl + step) & (ZL - 1)
         for j in range(DEPTH):
-            part = source.at[:, j * ROWS_HERE : (j + 1) * ROWS_HERE]
-            copies.append(pltpu.make_async_copy(part, held.at[j, :, c], sems.at[len(copies)]))
-        copies.append(pltpu.make_async_copy(source.at[:, FULL:], came.at[:, c], sems.at[len(copies)]))
+            part = source.at[:, :, j * ROWS_HERE : (j + 1) * ROWS_HERE]
+            copies.append(pltpu.make_async_copy(part, held.at[j, xs, there, :, c], sems.at[len(copies)]))
+        copies.append(pltpu.make_async_copy(source.at[:, :, FULL:], came.at[xs, there, :, c], sems.at[len(copies)]))
     for copy in copies:
         copy.start()
     for copy in copies:
@@ -141,21 +138,21 @@
     pl.when(zp == 1)(lambda: run(1))
 
 
-def select(lists, here, there):
+def select(lists, pieces):
     return pl.pallas_call(
         select_kernel,
         out_shape=pltpu.VMEM((DESTS, COUNT, TILE, BLK), jnp.bfloat16),
-        in_specs=[SMEM, VMEM, VMEM],
+        in_specs=[SMEM] + [VMEM] * (2 * len(PARTS)),
         out_specs=VMEM,
         scratch_shapes=[
-            pltpu.VMEM((DEPTH, OWNERS, CORE, ROWS_HERE, TILE, BLK), jnp.bfloat16),
-            pltpu.VMEM((OWNERS, CORE, ROWS_HERE // 2, TILE, BLK), jnp.bfloat16),
+            pltpu.VMEM((DEPTH, X, ZL, ZP, CORE, ROWS_HERE, TILE, BLK), jnp.bfloat16),
+            pltpu.VMEM((X, ZL, ZP, CORE, ROWS_HERE // 2, TILE, BLK), jnp.bfloat16),
             pltpu.VMEM((PAIRS, 2, TILE, BLK), jnp.bfloat16),
-            pltpu.SemaphoreType.DMA((CORE * (DEPTH + 1),)),
+            pltpu.SemaphoreType.DMA((CORE * len(PARTS) * (DEPTH + 1),)),
         ],
         compiler_params=pltpu.CompilerParams(vmem_limit_bytes=12 * MIB),
         name="select",
-    )(lists, near(here), near(there))
+    )(lists, *(near(p) for p in pieces))
 
 
 def groups():
@@ -259,12 +256,20 @@
     )(*(near(p) for p in (strips, *parts)))
 
 
+def shifted(value, step):
+    return lax.ppermute(value, "zl", [((i + step) % ZL, i) for i in range(ZL)])
+
+
 def body(column_lists, block_values):
     lists = column_lists.T
-    mine = pack(block_values).reshape(OWNERS, MESSAGE, TILE, BLK)
-    here = lax.all_to_all(mine, ("x", "zl", "zp"), 0, 0, tiled=True)
-    there = lax.ppermute(here, "core", [(0, 1), (1, 0)])
-    asked = select(lists, here, there)
+    mine = pack(block_values).reshape(X * ZP, MESSAGE, TILE, BLK)
+    part = lax.all_to_all(mine, ("x", "zp"), 0, 0, tiled=True).reshape(X, ZP, MESSAGE, TILE, BLK)
+    ahead, behind = shifted(part, 1), shifted(part, -1)
+    far = shifted(ahead[: X // 2], 1), shifted(behind[X // 2 :], -1)
+    here = [part, ahead, behind, *far]
+    near_pieces = lax.optimization_barrier((ahead, behind))
+    there = [lax.ppermute(p, "core", [(0, 1), (1, 0)]) for p in (part, *near_pieces, *far)]
+    asked = select(lists, here + there)
     got = lax.all_to_all(asked, ("x", "zp", "y"), 0, 0, tiled=True)
     strips = purify(lists, got, block_values)
     two, one, three = (

time: 88.9 us -> 88.2 us (level)
  the two profiles are of different devices: /device:TPU:8 before, /device:TPU:64 now
where the time goes in v8:
time: 88.2 us; the launch traced here: 88 us
  blocking collectives  44.6 us (51%)
  waiting for transfers between devices  22.4 us (25%)
  starting transfers between devices  13.1 us (15%)
  Pallas kernels  7.81 us (9%)
    all_to_all x1, blocking collectives, body(): got = lax.all_to_all(asked, ('x', 'zp', 'y'), 0, 0, tiled=True)  32 us
    ppermute x4, waiting for transfers between devices, shifted(): return lax.ppermute(value, 'zl', [((i + step) % ZL, i) for i in range(ZL)])  15.5 us
    all_to_all x1, blocking collectives, body(): lax.all_to_all(mine, ('x', 'zp'), 0, 0, tiled=True)  12.6 us
    ppermute x4, starting transfers between devices, shifted(): return lax.ppermute(value, 'zl', [((i + step) % ZL, i) for i in range(ZL)])  8.34 us
    ppermute x3, waiting for transfers between devices, body(): lax.ppermute(strips[n], 'y', [(i, (i + n) % Y) for i in range(Y)])  5.62 us
    ppermute x3, starting transfers between devices, body(): lax.ppermute(strips[n], 'y', [(i, (i + n) % Y) for i in range(Y)])  4.14 us
    pallas_call x1, Pallas kernels, select(): pl.pallas_call(select_kernel, out_shape=pltpu.VMEM((DESTS, COUNT, TILE, B...  3.08 us
    pallas_call x1, Pallas kernels, purify(): pl.pallas_call(purify_kernel, out_shape=pltpu.VMEM((Y, SLOTS, BLK // Y, B...  2.72 us
  transfers between devices with their start and end apart: 12, of which 8 were waited for; matrix products, arithmetic and copies ran while one was open for 0% of the time, Pallas kernels for 0%

profile of v8, /device:TPU:64, one launch (start us, length us, event | category | flops | bytes accessed | tf_op | source)
XLA Modules:
  0.0 88.0 jit_solution(7961028060828014355)
XLA Ops:
  0.0 1.2 %pack.1 = bf16[4,2,14,8,128]{4,3,2,1,0:T(8,128)(2,1)S(1)} custom-call(bf16[4,13,128,128]{3,2,1,0:T(8,128)(2,1)} %own.1), custom_call_target="tpu_custom_call" | custom-call | tf_op jit(solution)/shard_map/pack/pallas_call | solution.py:84
  1.2 12.6 %all_to_all.10 = bf16[8,14,8,128]{3,2,1,0:T(8,128)(2,1)S(1)} all-to-all(bf16[8,14,8,128]{3,2,1,0:T(8,128)(2,1)S(1)} %bitcast.14), channel_id=1, replica_groups=mesh['x'=4,'zl'=4,'zp'=2,'core'=2,'y'=4] {'x','zp'}, dimensions={0} | all-to-all | bytes 458752 | tf_op jit(solution)/shard_map/all_to_all | solution.py:266
  13.8 3.6 %collective-permute-start.1 = (bf16[4,2,14,8,128]{4,3,2,1,0:T(8,128)(2,1)S(1)}, bf16[4,2,14,8,128]{4,3,2,1,0:T(8,128)(2,1)S(1)}, u32[]{:S(2)}, u32[]{:S(2)}) collective-permute-start(bf16[4,2,14,8,128]{4,3,2,1,0:T(8,128)(2,1)S(1)} %bitcast.10), channel_id=1, source_target_pairs={{48,0},{0,16},{16,32},{32,48},{49,1},{1,17},{17,33},{33,49},{50,2}... | collective-permute-start | bytes 688136 | tf_op jit(solution)/shard_map/ppermute | solution.py:260
  17.4 7.6 %collective-permute-done.1.refs_2_ = bf16[4,2,14,8,128]{4,3,2,1,0:T(8,128)(2,1)S(1)} collective-permute-done((bf16[4,2,14,8,128]{4,3,2,1,0:T(8,128)(2,1)S(1)}, bf16[4,2,14,8,128]{4,3,2,1,0:T(8,128)(2,1)S(1)}, u32[]{:S(2)}, u32[]{:S(2)}) %collective-permute-start.1) | collective-permute-done | bytes 229408 | tf_op jit(solution)/shard_map/ppermute | solution.py:260
  25.0 4.7 %collective-permute-start.3 = (bf16[2,2,14,8,128]{4,3,2,1,0:T(8,128)(2,1)S(1)}, bf16[2,2,14,8,128]{4,3,2,1,0:T(8,128)(2,1)S(1)}, u32[]{:S(2)}, u32[]{:S(2)}) collective-permute-start(bf16[2,2,14,8,128]{4,3,2,1,0:T(8,128)(2,1)S(1)} %slice.21), channel_id=1, source_target_pairs={{48,0},{0,16},{16,32},{32,48},{49,1},{1,17},{17,33},{33,49},{50,2}... | collective-permute-start | bytes 344072 | tf_op jit(solution)/shard_map/ppermute | solution.py:260
  29.7 0.3 collective-permute-done.refs_1_
  30.0 0.1 collective-permute-start.2
  30.1 0.1 collective-permute-start.5
  30.2 0.5 collective-permute-start.6
  30.7 1.6 %collective-permute-done.3.refs_4_ = bf16[2,2,14,8,128]{4,3,2,1,0:T(8,128)(2,1)S(1)} collective-permute-done((bf16[2,2,14,8,128]{4,3,2,1,0:T(8,128)(2,1)S(1)}, bf16[2,2,14,8,128]{4,3,2,1,0:T(8,128)(2,1)S(1)}, u32[]{:S(2)}, u32[]{:S(2)}) %collective-permute-start.3) | collective-permute-done | bytes 114720 | tf_op jit(solution)/shard_map/ppermute | solution.py:260
  32.3 0.0 collective-permute-start.8
  32.3 6.0 %collective-permute-done.2.refs_3_ = bf16[2,2,14,8,128]{4,3,2,1,0:T(8,128)(2,1)S(1)} collective-permute-done((bf16[2,2,14,8,128]{4,3,2,1,0:T(8,128)(2,1)S(1)}, bf16[2,2,14,8,128]{4,3,2,1,0:T(8,128)(2,1)S(1)}, u32[]{:S(2)}, u32[]{:S(2)}) %collective-permute-start.2) | collective-permute-done | bytes 114720 | tf_op jit(solution)/shard_map/ppermute | solution.py:260
  38.3 1.3 %collective-permute-done.7.refs_8_ = bf16[2,2,14,8,128]{4,3,2,1,0:T(8,128)(2,1)S(1)} collective-permute-done((bf16[2,2,14,8,128]{4,3,2,1,0:T(8,128)(2,1)S(1)}, bf16[2,2,14,8,128]{4,3,2,1,0:T(8,128)(2,1)S(1)}, u32[]{:S(2)}, u32[]{:S(2)}) %collective-permute-start.7) | collective-permute-done | bytes 114720 | tf_op jit(solution)/shard_map/ppermute | solution.py:271
  39.6 3.1 %select.1 = bf16[32,29,8,128]{3,2,1,0:T(8,128)(2,1)S(1)} custom-call(s32[13,256]{1,0:T(8,128)S(1)} %bitcast.15, bf16[4,2,14,8,128]{4,3,2,1,0:T(8,128)(2,1)S(1)} %bitcast.13, bf16[4,2,14,8,128]{4,3,2,1,0:T(8,128)(2,1)S(1)} %collective-permute-done.refs_1_, bf16[4,2,14,8,128]{4,3,2,1,0:T(8,128)(2,1)S(1)} %collective-permute-done.1.refs_2_, ...), custom_call_target="tpu_custom_call" | custom-call | tf_op jit(solution)/shard_map/select/pallas_call | solution.py:142
  42.7 0.0 copy-start
  42.7 32.0 %all_to_all.11.got = bf16[32,29,8,128]{3,2,1,0:T(8,128)(2,1)S(1)} all-to-all(bf16[32,29,8,128]{3,2,1,0:T(8,128)(2,1)S(1)} %select.1), channel_id=1, replica_groups=mesh['x'=4,'zl'=4,'zp'=2,'core'=2,'y'=4] {'x','zp','y'}, dimensions={0} | all-to-all | bytes 3801088 | tf_op jit(solution)/shard_map/all_to_all | solution.py:273
  74.7 2.7 %purify.1.own = bf16[4,13,32,128]{3,2,1,0:T(8,128)(2,1)S(1)} custom-call(s32[13,256]{1,0:T(8,128)S(1)} %bitcast.16, bf16[32,29,8,128]{3,2,1,0:T(8,128)(2,1)S(1)} %all_to_all.11.got, bf16[4,13,128,128]{3,2,1,0:T(8,128)(2,1)S(1)} %copy-done), custom_call_target="tpu_custom_call" | custom-call | tf_op jit(solution)/shard_map/purify/pallas_call | solution.py:223
  77.5 1.5 %collective-permute-start.11 = (bf16[13,32,128]{2,1,0:T(8,128)(2,1)S(1)}, bf16[13,32,128]{2,1,0:T(8,128)(2,1)S(1)}, u32[]{:S(2)}, u32[]{:S(2)}) collective-permute-start(bf16[13,32,128]{2,1,0:T(8,128)(2,1)S(1)} %get-tuple-element.9), channel_id=1, source_target_pairs={{0,3},{1,0},{2,1},{3,2},{4,7},{5,4},{6,5},{7,6},{8,11},{9,8},{10,9... | collective-permute-start | bytes 319496 | tf_op jit(solution)/shard_map/ppermute | solution.py:276
  79.0 2.4 %collective-permute-start.10 = (bf16[13,32,128]{2,1,0:T(8,128)(2,1)S(1)}, bf16[13,32,128]{2,1,0:T(8,128)(2,1)S(1)}, u32[]{:S(2)}, u32[]{:S(2)}) collective-permute-start(bf16[13,32,128]{2,1,0:T(8,128)(2,1)S(1)} %get-tuple-element.10), channel_id=1, source_target_pairs={{0,2},{1,3},{2,0},{3,1},{4,6},{5,7},{6,4},{7,5},{8,10},{9,11},{10,... | collective-permute-start | bytes 319496 | tf_op jit(solution)/shard_map/ppermute | solution.py:276
  81.3 0.3 collective-permute-start.9
  81.6 1.6 %collective-permute-done.11.three = bf16[13,32,128]{2,1,0:T(8,128)(2,1)S(1)} collective-permute-done((bf16[13,32,128]{2,1,0:T(8,128)(2,1)S(1)}, bf16[13,32,128]{2,1,0:T(8,128)(2,1)S(1)}, u32[]{:S(2)}, u32[]{:S(2)}) %collective-permute-start.11) | collective-permute-done | bytes 106528 | tf_op jit(solution)/shard_map/ppermute | solution.py:276
  83.2 2.1 %collective-permute-done.10.two = bf16[13,32,128]{2,1,0:T(8,128)(2,1)S(1)} collective-permute-done((bf16[13,32,128]{2,1,0:T(8,128)(2,1)S(1)}, bf16[13,32,128]{2,1,0:T(8,128)(2,1)S(1)}, u32[]{:S(2)}, u32[]{:S(2)}) %collective-permute-start.10) | collective-permute-done | bytes 106528 | tf_op jit(solution)/shard_map/ppermute | solution.py:276
  85.3 2.0 %collective-permute-done.9.one = bf16[13,32,128]{2,1,0:T(8,128)(2,1)S(1)} collective-permute-done((bf16[13,32,128]{2,1,0:T(8,128)(2,1)S(1)}, bf16[13,32,128]{2,1,0:T(8,128)(2,1)S(1)}, u32[]{:S(2)}, u32[]{:S(2)}) %collective-permute-start.9) | collective-permute-done | bytes 106528 | tf_op jit(solution)/shard_map/ppermute | solution.py:276
  87.2 0.8 place.1
  (13 shorter events, 0.1 us)
Async XLA Ops:
  0.0 39.6 %copy-start.1 = (s32[256,13]{0,1:T(8,128)S(1)}, s32[256,13]{0,1:T(8,128)}, u32[]{:S(2)}) copy-start(s32[256,13]{0,1:T(8,128)} %param.2) | copy-start | bytes 39940
  13.8 11.2 %collective-permute-start.1 = (bf16[4,2,14,8,128]{4,3,2,1,0:T(8,128)(2,1)S(1)}, bf16[4,2,14,8,128]{4,3,2,1,0:T(8,128)(2,1)S(1)}, u32[]{:S(2)}, u32[]{:S(2)}) collective-permute-start(bf16[4,2,14,8,128]{4,3,2,1,0:T(8,128)(2,1)S(1)} %bitcast.10), channel_id=1, source_target_pairs={{48,0},{0,16},{16,32},{32,48},{49,1},{1,17},{17,33},{33,49},{50,2}... | collective-permute-start | bytes 688136 | tf_op jit(solution)/shard_map/ppermute | solution.py:260
  17.4 12.7 %collective-permute-start = (bf16[4,2,14,8,128]{4,3,2,1,0:T(8,128)(2,1)S(1)}, bf16[4,2,14,8,128]{4,3,2,1,0:T(8,128)(2,1)S(1)}, u32[]{:S(2)}, u32[]{:S(2)}) collective-permute-start(bf16[4,2,14,8,128]{4,3,2,1,0:T(8,128)(2,1)S(1)} %bitcast.11), channel_id=1, source_target_pairs={{16,0},{32,16},{48,32},{0,48},{17,1},{33,17},{49,33},{1,49},{18,2}... | collective-permute-start | bytes 688136 | tf_op jit(solution)/shard_map/ppermute | solution.py:260
  17.4 20.9 %collective-permute-start.4 = (bf16[4,2,14,8,128]{4,3,2,1,0:T(8,128)(2,1)S(1)}, bf16[4,2,14,8,128]{4,3,2,1,0:T(8,128)(2,1)S(1)}, u32[]{:S(2)}, u32[]{:S(2)}) collective-permute-start(bf16[4,2,14,8,128]{4,3,2,1,0:T(8,128)(2,1)S(1)} %bitcast.12), channel_id=1, source_target_pairs={{0,4},{4,0},{1,5},{5,1},{2,6},{6,2},{3,7},{7,3},{8,12},{12,8},{9,1... | collective-permute-start | bytes 688136 | tf_op jit(solution)/shard_map/ppermute | solution.py:271
  25.0 7.3 %collective-permute-start.3 = (bf16[2,2,14,8,128]{4,3,2,1,0:T(8,128)(2,1)S(1)}, bf16[2,2,14,8,128]{4,3,2,1,0:T(8,128)(2,1)S(1)}, u32[]{:S(2)}, u32[]{:S(2)}) collective-permute-start(bf16[2,2,14,8,128]{4,3,2,1,0:T(8,128)(2,1)S(1)} %slice.21), channel_id=1, source_target_pairs={{48,0},{0,16},{16,32},{32,48},{49,1},{1,17},{17,33},{33,49},{50,2}... | collective-permute-start | bytes 344072 | tf_op jit(solution)/shard_map/ppermute | solution.py:260
  30.0 8.2 %collective-permute-start.2 = (bf16[2,2,14,8,128]{4,3,2,1,0:T(8,128)(2,1)S(1)}, bf16[2,2,14,8,128]{4,3,2,1,0:T(8,128)(2,1)S(1)}, u32[]{:S(2)}, u32[]{:S(2)}) collective-permute-start(bf16[2,2,14,8,128]{4,3,2,1,0:T(8,128)(2,1)S(1)} %slice.20), channel_id=1, source_target_pairs={{16,0},{32,16},{48,32},{0,48},{17,1},{33,17},{49,33},{1,49},{18,2}... | collective-permute-start | bytes 344072 | tf_op jit(solution)/shard_map/ppermute | solution.py:260
  30.1 9.4 %collective-permute-start.5 = (bf16[4,2,14,8,128]{4,3,2,1,0:T(8,128)(2,1)S(1)}, bf16[4,2,14,8,128]{4,3,2,1,0:T(8,128)(2,1)S(1)}, u32[]{:S(2)}, u32[]{:S(2)}) collective-permute-start(bf16[4,2,14,8,128]{4,3,2,1,0:T(8,128)(2,1)S(1)} %collective-permute-done.refs_1_), channel_id=1, source_target_pairs={{0,4},{4,0},{1,5},{5,1},{2,6},{6,2},{3,7},{7,3},{8,12},{12,8},{9,1... | collective-permute-start | bytes 688136 | tf_op jit(solution)/shard_map/ppermute | solution.py:271
  30.2 9.3 %collective-permute-start.6 = (bf16[4,2,14,8,128]{4,3,2,1,0:T(8,128)(2,1)S(1)}, bf16[4,2,14,8,128]{4,3,2,1,0:T(8,128)(2,1)S(1)}, u32[]{:S(2)}, u32[]{:S(2)}) collective-permute-start(bf16[4,2,14,8,128]{4,3,2,1,0:T(8,128)(2,1)S(1)} %collective-permute-done.1.refs_2_), channel_id=1, source_target_pairs={{0,4},{4,0},{1,5},{5,1},{2,6},{6,2},{3,7},{7,3},{8,12},{12,8},{9,1... | collective-permute-start | bytes 688136 | tf_op jit(solution)/shard_map/ppermute | solution.py:271
  32.3 6.0 %collective-permute-start.8 = (bf16[2,2,14,8,128]{4,3,2,1,0:T(8,128)(2,1)S(1)}, bf16[2,2,14,8,128]{4,3,2,1,0:T(8,128)(2,1)S(1)}, u32[]{:S(2)}, u32[]{:S(2)}) collective-permute-start(bf16[2,2,14,8,128]{4,3,2,1,0:T(8,128)(2,1)S(1)} %collective-permute-done.3.refs_4_), channel_id=1, source_target_pairs={{0,4},{4,0},{1,5},{5,1},{2,6},{6,2},{3,7},{7,3},{8,12},{12,8},{9,1... | collective-permute-start | bytes 344072 | tf_op jit(solution)/shard_map/ppermute | solution.py:271
  38.3 1.3 %collective-permute-start.7 = (bf16[2,2,14,8,128]{4,3,2,1,0:T(8,128)(2,1)S(1)}, bf16[2,2,14,8,128]{4,3,2,1,0:T(8,128)(2,1)S(1)}, u32[]{:S(2)}, u32[]{:S(2)}) collective-permute-start(bf16[2,2,14,8,128]{4,3,2,1,0:T(8,128)(2,1)S(1)} %collective-permute-done.2.refs_3_), channel_id=1, source_target_pairs={{0,4},{4,0},{1,5},{5,1},{2,6},{6,2},{3,7},{7,3},{8,12},{12,8},{9,1... | collective-permute-start | bytes 344072 | tf_op jit(solution)/shard_map/ppermute | solution.py:271
  42.7 32.0 %copy-start = (bf16[4,13,128,128]{3,2,1,0:T(8,128)(2,1)S(1)}, bf16[4,13,128,128]{3,2,1,0:T(8,128)(2,1)}, u32[]{:S(2)}) copy-start(bf16[4,13,128,128]{3,2,1,0:T(8,128)(2,1)} %own.1) | copy-start | bytes 5111812
  77.5 5.7 %collective-permute-start.11 = (bf16[13,32,128]{2,1,0:T(8,128)(2,1)S(1)}, bf16[13,32,128]{2,1,0:T(8,128)(2,1)S(1)}, u32[]{:S(2)}, u32[]{:S(2)}) collective-permute-start(bf16[13,32,128]{2,1,0:T(8,128)(2,1)S(1)} %get-tuple-element.9), channel_id=1, source_target_pairs={{0,3},{1,0},{2,1},{3,2},{4,7},{5,4},{6,5},{7,6},{8,11},{9,8},{10,9... | collective-permute-start | bytes 319496 | tf_op jit(solution)/shard_map/ppermute | solution.py:276
  79.0 6.3 %collective-permute-start.10 = (bf16[13,32,128]{2,1,0:T(8,128)(2,1)S(1)}, bf16[13,32,128]{2,1,0:T(8,128)(2,1)S(1)}, u32[]{:S(2)}, u32[]{:S(2)}) collective-permute-start(bf16[13,32,128]{2,1,0:T(8,128)(2,1)S(1)} %get-tuple-element.10), channel_id=1, source_target_pairs={{0,2},{1,3},{2,0},{3,1},{4,6},{5,7},{6,4},{7,5},{8,10},{9,11},{10,... | collective-permute-start | bytes 319496 | tf_op jit(solution)/shard_map/ppermute | solution.py:276
  81.3 5.9 %collective-permute-start.9 = (bf16[13,32,128]{2,1,0:T(8,128)(2,1)S(1)}, bf16[13,32,128]{2,1,0:T(8,128)(2,1)S(1)}, u32[]{:S(2)}, u32[]{:S(2)}) collective-permute-start(bf16[13,32,128]{2,1,0:T(8,128)(2,1)S(1)} %get-tuple-element.11), channel_id=1, source_target_pairs={{0,1},{1,2},{2,3},{3,0},{4,5},{5,6},{6,7},{7,4},{8,9},{9,10},{10,1... | collective-permute-start | bytes 319496 | tf_op jit(solution)/shard_map/ppermute | solution.py:276

commit v9 on v8

--- a/solution.py
+++ b/solution.py
@@ -168,7 +168,8 @@
 GROUPS = groups()
 
 
-def purify_kernel(lists, got, own, out, w, sq):
+def purify_kernel(lists, got, own, *refs):
+    outs, (w, sq, out) = refs[:Y], refs[Y:]
     x, zl, zp, core, y = (lax.axis_index(a) for a in AXES)
     row = ROWS_HERE * ((x * Z + 2 * zl + zp) * CORE + core) + y
 
@@ -216,18 +217,21 @@
             value = 3.0 * sq[:, blk(s + j)].astype(jnp.float32) - 2.0 * total[:, blk(j)]
             value = mask(value, s + j).T.astype(jnp.bfloat16)
             for part in range(Y):
-                out[(part - y) & (Y - 1), s + j] = value[part * (BLK // Y) : (part + 1) * (BLK // Y)]
+                out[part, s + j] = value[part * (BLK // Y) : (part + 1) * (BLK // Y)]
+    for n in range(Y):
+        outs[n][...] = out[(y + n) & (Y - 1)]
 
 
 def purify(lists, got, own):
     return pl.pallas_call(
         purify_kernel,
-        out_shape=pltpu.VMEM((Y, SLOTS, BLK // Y, BLK), jnp.bfloat16),
+        out_shape=[pltpu.VMEM((SLOTS, BLK // Y, BLK), jnp.bfloat16)] * Y,
         in_specs=[SMEM, VMEM, VMEM],
-        out_specs=VMEM,
+        out_specs=[VMEM] * Y,
         scratch_shapes=[
             pltpu.VMEM((SLOTS * BLK, SLOTS * BLK), jnp.bfloat16),
             pltpu.VMEM((BLK, SLOTS * BLK), jnp.bfloat16),
+            pltpu.VMEM((Y, SLOTS, BLK // Y, BLK), jnp.bfloat16),
         ],
         compiler_params=pltpu.CompilerParams(vmem_limit_bytes=24 * MIB),
         name="purify",
@@ -236,7 +240,7 @@
 
 def place_kernel(own, one, two, three, out, sems):
     y = lax.axis_index("y")
-    parts = (own.at[0], one, two, three)
+    parts = (own, one, two, three)
     copies = [pltpu.make_async_copy(part, out.at[(y - n) & (Y - 1)], sems.at[n]) for n, part in enumerate(parts)]
     for copy in copies:
         copy.start()
@@ -275,7 +279,7 @@
     two, one, three = (
         lax.ppermute(strips[n], "y", [(i, (i + n) % Y) for i in range(Y)]) for n in (2, 1, 3)
     )
-    mixed = place(strips, (one, two, three))
+    mixed = place(strips[0], (one, two, three))
     return mixed.transpose(0, 1, 3, 2)
 
 

time: 88.2 us -> 86.9 us (0.985)
  the two profiles are of different devices: /device:TPU:64 before, /device:TPU:8 now
where the time goes in v9:
time: 86.9 us; the launch traced here: 86 us
  blocking collectives  44.7 us (51%)
  waiting for transfers between devices  19.9 us (23%)
  starting transfers between devices  13.6 us (16%)
  Pallas kernels  7.83 us (9%)
    all_to_all x1, blocking collectives, body(): got = lax.all_to_all(asked, ('x', 'zp', 'y'), 0, 0, tiled=True)  32.1 us
    ppermute x4, waiting for transfers between devices, shifted(): return lax.ppermute(value, 'zl', [((i + step) % ZL, i) for i in range(ZL)])  13.6 us
    all_to_all x1, blocking collectives, body(): lax.all_to_all(mine, ('x', 'zp'), 0, 0, tiled=True)  12.6 us
    ppermute x4, starting transfers between devices, shifted(): return lax.ppermute(value, 'zl', [((i + step) % ZL, i) for i in range(ZL)])  9.78 us
    ppermute x3, waiting for transfers between devices, body(): lax.ppermute(strips[n], 'y', [(i, (i + n) % Y) for i in range(Y)])  5.03 us
    ppermute x3, starting transfers between devices, body(): lax.ppermute(strips[n], 'y', [(i, (i + n) % Y) for i in range(Y)])  3.28 us
    pallas_call x1, Pallas kernels, select(): pl.pallas_call(select_kernel, out_shape=pltpu.VMEM((DESTS, COUNT, TILE, B...  3.08 us
    pallas_call x1, Pallas kernels, purify(): pl.pallas_call(purify_kernel, out_shape=[pltpu.VMEM((SLOTS, BLK // Y, BLK...  2.75 us
  transfers between devices with their start and end apart: 12, of which 8 were waited for; matrix products, arithmetic and copies ran while one was open for 0% of the time, Pallas kernels for 0%

profile of v9, /device:TPU:8, one launch (start us, length us, event | category | flops | bytes accessed | tf_op | source)
XLA Modules:
  0.0 86.0 jit_solution(17019697610406919685)
XLA Ops:
  0.0 1.2 %pack.1 = bf16[4,2,14,8,128]{4,3,2,1,0:T(8,128)(2,1)S(1)} custom-call(bf16[4,13,128,128]{3,2,1,0:T(8,128)(2,1)} %own.1), custom_call_target="tpu_custom_call" | custom-call | tf_op jit(solution)/shard_map/pack/pallas_call | solution.py:84
  1.2 12.6 %all_to_all.10 = bf16[8,14,8,128]{3,2,1,0:T(8,128)(2,1)S(1)} all-to-all(bf16[8,14,8,128]{3,2,1,0:T(8,128)(2,1)S(1)} %bitcast.8), channel_id=1, replica_groups=mesh['x'=4,'zl'=4,'zp'=2,'core'=2,'y'=4] {'x','zp'}, dimensions={0} | all-to-all | bytes 458752 | tf_op jit(solution)/shard_map/all_to_all | solution.py:270
  13.8 3.3 %collective-permute-start.1 = (bf16[4,2,14,8,128]{4,3,2,1,0:T(8,128)(2,1)S(1)}, bf16[4,2,14,8,128]{4,3,2,1,0:T(8,128)(2,1)S(1)}, u32[]{:S(2)}, u32[]{:S(2)}) collective-permute-start(bf16[4,2,14,8,128]{4,3,2,1,0:T(8,128)(2,1)S(1)} %bitcast.4), channel_id=1, source_target_pairs={{48,0},{0,16},{16,32},{32,48},{49,1},{1,17},{17,33},{33,49},{50,2}... | collective-permute-start | bytes 688136 | tf_op jit(solution)/shard_map/ppermute | solution.py:264
  17.1 2.1 %collective-permute-start = (bf16[4,2,14,8,128]{4,3,2,1,0:T(8,128)(2,1)S(1)}, bf16[4,2,14,8,128]{4,3,2,1,0:T(8,128)(2,1)S(1)}, u32[]{:S(2)}, u32[]{:S(2)}) collective-permute-start(bf16[4,2,14,8,128]{4,3,2,1,0:T(8,128)(2,1)S(1)} %bitcast.5), channel_id=1, source_target_pairs={{16,0},{32,16},{48,32},{0,48},{17,1},{33,17},{49,33},{1,49},{18,2}... | collective-permute-start | bytes 688136 | tf_op jit(solution)/shard_map/ppermute | solution.py:264
  19.2 7.6 %collective-permute-done.1.refs_2_ = bf16[4,2,14,8,128]{4,3,2,1,0:T(8,128)(2,1)S(1)} collective-permute-done((bf16[4,2,14,8,128]{4,3,2,1,0:T(8,128)(2,1)S(1)}, bf16[4,2,14,8,128]{4,3,2,1,0:T(8,128)(2,1)S(1)}, u32[]{:S(2)}, u32[]{:S(2)}) %collective-permute-start.1) | collective-permute-done | bytes 229408 | tf_op jit(solution)/shard_map/ppermute | solution.py:264
  26.8 1.6 %collective-permute-start.3 = (bf16[2,2,14,8,128]{4,3,2,1,0:T(8,128)(2,1)S(1)}, bf16[2,2,14,8,128]{4,3,2,1,0:T(8,128)(2,1)S(1)}, u32[]{:S(2)}, u32[]{:S(2)}) collective-permute-start(bf16[2,2,14,8,128]{4,3,2,1,0:T(8,128)(2,1)S(1)} %slice.9), channel_id=1, source_target_pairs={{48,0},{0,16},{16,32},{32,48},{49,1},{1,17},{17,33},{33,49},{50,2}... | collective-permute-start | bytes 344072 | tf_op jit(solution)/shard_map/ppermute | solution.py:264
  28.4 1.2 %collective-permute-done.refs_1_ = bf16[4,2,14,8,128]{4,3,2,1,0:T(8,128)(2,1)S(1)} collective-permute-done((bf16[4,2,14,8,128]{4,3,2,1,0:T(8,128)(2,1)S(1)}, bf16[4,2,14,8,128]{4,3,2,1,0:T(8,128)(2,1)S(1)}, u32[]{:S(2)}, u32[]{:S(2)}) %collective-permute-start) | collective-permute-done | bytes 229408 | tf_op jit(solution)/shard_map/ppermute | solution.py:264
  29.6 2.8 %collective-permute-start.2 = (bf16[2,2,14,8,128]{4,3,2,1,0:T(8,128)(2,1)S(1)}, bf16[2,2,14,8,128]{4,3,2,1,0:T(8,128)(2,1)S(1)}, u32[]{:S(2)}, u32[]{:S(2)}) collective-permute-start(bf16[2,2,14,8,128]{4,3,2,1,0:T(8,128)(2,1)S(1)} %slice.8), channel_id=1, source_target_pairs={{16,0},{32,16},{48,32},{0,48},{17,1},{33,17},{49,33},{1,49},{18,2}... | collective-permute-start | bytes 344072 | tf_op jit(solution)/shard_map/ppermute | solution.py:264
  32.3 0.5 collective-permute-start.6
  32.8 1.8 %collective-permute-done.3.refs_4_ = bf16[2,2,14,8,128]{4,3,2,1,0:T(8,128)(2,1)S(1)} collective-permute-done((bf16[2,2,14,8,128]{4,3,2,1,0:T(8,128)(2,1)S(1)}, bf16[2,2,14,8,128]{4,3,2,1,0:T(8,128)(2,1)S(1)}, u32[]{:S(2)}, u32[]{:S(2)}) %collective-permute-start.3) | collective-permute-done | bytes 114720 | tf_op jit(solution)/shard_map/ppermute | solution.py:264
  34.6 0.0 collective-permute-start.8
  34.6 3.1 %collective-permute-done.2.refs_3_ = bf16[2,2,14,8,128]{4,3,2,1,0:T(8,128)(2,1)S(1)} collective-permute-done((bf16[2,2,14,8,128]{4,3,2,1,0:T(8,128)(2,1)S(1)}, bf16[2,2,14,8,128]{4,3,2,1,0:T(8,128)(2,1)S(1)}, u32[]{:S(2)}, u32[]{:S(2)}) %collective-permute-start.2) | collective-permute-done | bytes 114720 | tf_op jit(solution)/shard_map/ppermute | solution.py:264
  37.7 1.3 %collective-permute-done.7.refs_8_ = bf16[2,2,14,8,128]{4,3,2,1,0:T(8,128)(2,1)S(1)} collective-permute-done((bf16[2,2,14,8,128]{4,3,2,1,0:T(8,128)(2,1)S(1)}, bf16[2,2,14,8,128]{4,3,2,1,0:T(8,128)(2,1)S(1)}, u32[]{:S(2)}, u32[]{:S(2)}) %collective-permute-start.7) | collective-permute-done | bytes 114720 | tf_op jit(solution)/shard_map/ppermute | solution.py:275
  39.0 3.1 %select.1 = bf16[32,29,8,128]{3,2,1,0:T(8,128)(2,1)S(1)} custom-call(s32[13,256]{1,0:T(8,128)S(1)} %bitcast.9, bf16[4,2,14,8,128]{4,3,2,1,0:T(8,128)(2,1)S(1)} %bitcast.7, bf16[4,2,14,8,128]{4,3,2,1,0:T(8,128)(2,1)S(1)} %collective-permute-done.refs_1_, bf16[4,2,14,8,128]{4,3,2,1,0:T(8,128)(2,1)S(1)} %collective-permute-done.1.refs_2_, ...), custom_call_target="tpu_custom_call" | custom-call | tf_op jit(solution)/shard_map/select/pallas_call | solution.py:142
  42.1 0.0 copy-start
  42.1 32.1 %all_to_all.11.got = bf16[32,29,8,128]{3,2,1,0:T(8,128)(2,1)S(1)} all-to-all(bf16[32,29,8,128]{3,2,1,0:T(8,128)(2,1)S(1)} %select.1), channel_id=1, replica_groups=mesh['x'=4,'zl'=4,'zp'=2,'core'=2,'y'=4] {'x','zp','y'}, dimensions={0} | all-to-all | bytes 3801088 | tf_op jit(solution)/shard_map/all_to_all | solution.py:277
  74.2 2.7 %purify.1 = (bf16[13,32,128]{2,1,0:T(8,128)(2,1)S(1)}, bf16[13,32,128]{2,1,0:T(8,128)(2,1)S(1)}, bf16[13,32,128]{2,1,0:T(8,128)(2,1)S(1)}, bf16[13,32,128]{2,1,0:T(8,128)(2,1)S(1)}) custom-call(s32[13,256]{1,0:T(8,128)S(1)} %bitcast.10, bf16[32,29,8,128]{3,2,1,0:T(8,128)(2,1)S(1)} %all_to_all.11.got, bf16[4,13,128,128]{3,2,1,0:T(8,128)(2,1)S(1)} %copy-done), custom_call_target="tpu_custom_call" | custom-call | tf_op jit(solution)/shard_map/purify/pallas_call | solution.py:226
  77.0 1.0 %collective-permute-start.9 = (bf16[13,32,128]{2,1,0:T(8,128)(2,1)S(1)}, bf16[13,32,128]{2,1,0:T(8,128)(2,1)S(1)}, u32[]{:S(2)}, u32[]{:S(2)}) collective-permute-start(bf16[13,32,128]{2,1,0:T(8,128)(2,1)S(1)} %get-tuple-element.14), channel_id=1, source_target_pairs={{0,1},{1,2},{2,3},{3,0},{4,5},{5,6},{6,7},{7,4},{8,9},{9,10},{10,1... | collective-permute-start | bytes 319496 | tf_op jit(solution)/shard_map/ppermute | solution.py:280
  77.9 1.5 %collective-permute-start.10 = (bf16[13,32,128]{2,1,0:T(8,128)(2,1)S(1)}, bf16[13,32,128]{2,1,0:T(8,128)(2,1)S(1)}, u32[]{:S(2)}, u32[]{:S(2)}) collective-permute-start(bf16[13,32,128]{2,1,0:T(8,128)(2,1)S(1)} %get-tuple-element.15), channel_id=1, source_target_pairs={{0,2},{1,3},{2,0},{3,1},{4,6},{5,7},{6,4},{7,5},{8,10},{9,11},{10,... | collective-permute-start | bytes 319496 | tf_op jit(solution)/shard_map/ppermute | solution.py:280
  79.4 0.8 collective-permute-start.11
  80.2 1.7 %collective-permute-done.9.one = bf16[13,32,128]{2,1,0:T(8,128)(2,1)S(1)} collective-permute-done((bf16[13,32,128]{2,1,0:T(8,128)(2,1)S(1)}, bf16[13,32,128]{2,1,0:T(8,128)(2,1)S(1)}, u32[]{:S(2)}, u32[]{:S(2)}) %collective-permute-start.9) | collective-permute-done | bytes 106528 | tf_op jit(solution)/shard_map/ppermute | solution.py:280
  82.0 2.4 %collective-permute-done.10.two = bf16[13,32,128]{2,1,0:T(8,128)(2,1)S(1)} collective-permute-done((bf16[13,32,128]{2,1,0:T(8,128)(2,1)S(1)}, bf16[13,32,128]{2,1,0:T(8,128)(2,1)S(1)}, u32[]{:S(2)}, u32[]{:S(2)}) %collective-permute-start.10) | collective-permute-done | bytes 106528 | tf_op jit(solution)/shard_map/ppermute | solution.py:280
  84.3 0.9 %collective-permute-done.11.three = bf16[13,32,128]{2,1,0:T(8,128)(2,1)S(1)} collective-permute-done((bf16[13,32,128]{2,1,0:T(8,128)(2,1)S(1)}, bf16[13,32,128]{2,1,0:T(8,128)(2,1)S(1)}, u32[]{:S(2)}, u32[]{:S(2)}) %collective-permute-start.11) | collective-permute-done | bytes 106528 | tf_op jit(solution)/shard_map/ppermute | solution.py:280
  85.3 0.8 place.1
  (12 shorter events, 0.0 us)
Async XLA Ops:
  0.0 39.0 %copy-start.1 = (s32[256,13]{0,1:T(8,128)S(1)}, s32[256,13]{0,1:T(8,128)}, u32[]{:S(2)}) copy-start(s32[256,13]{0,1:T(8,128)} %param.2) | copy-start | bytes 39940
  13.8 13.0 %collective-permute-start.1 = (bf16[4,2,14,8,128]{4,3,2,1,0:T(8,128)(2,1)S(1)}, bf16[4,2,14,8,128]{4,3,2,1,0:T(8,128)(2,1)S(1)}, u32[]{:S(2)}, u32[]{:S(2)}) collective-permute-start(bf16[4,2,14,8,128]{4,3,2,1,0:T(8,128)(2,1)S(1)} %bitcast.4), channel_id=1, source_target_pairs={{48,0},{0,16},{16,32},{32,48},{49,1},{1,17},{17,33},{33,49},{50,2}... | collective-permute-start | bytes 688136 | tf_op jit(solution)/shard_map/ppermute | solution.py:264
  17.1 12.5 %collective-permute-start = (bf16[4,2,14,8,128]{4,3,2,1,0:T(8,128)(2,1)S(1)}, bf16[4,2,14,8,128]{4,3,2,1,0:T(8,128)(2,1)S(1)}, u32[]{:S(2)}, u32[]{:S(2)}) collective-permute-start(bf16[4,2,14,8,128]{4,3,2,1,0:T(8,128)(2,1)S(1)} %bitcast.5), channel_id=1, source_target_pairs={{16,0},{32,16},{48,32},{0,48},{17,1},{33,17},{49,33},{1,49},{18,2}... | collective-permute-start | bytes 688136 | tf_op jit(solution)/shard_map/ppermute | solution.py:264
  19.2 18.5 %collective-permute-start.4 = (bf16[4,2,14,8,128]{4,3,2,1,0:T(8,128)(2,1)S(1)}, bf16[4,2,14,8,128]{4,3,2,1,0:T(8,128)(2,1)S(1)}, u32[]{:S(2)}, u32[]{:S(2)}) collective-permute-start(bf16[4,2,14,8,128]{4,3,2,1,0:T(8,128)(2,1)S(1)} %bitcast.6), channel_id=1, source_target_pairs={{0,4},{4,0},{1,5},{5,1},{2,6},{6,2},{3,7},{7,3},{8,12},{12,8},{9,1... | collective-permute-start | bytes 688136 | tf_op jit(solution)/shard_map/ppermute | solution.py:275
  26.8 7.8 %collective-permute-start.3 = (bf16[2,2,14,8,128]{4,3,2,1,0:T(8,128)(2,1)S(1)}, bf16[2,2,14,8,128]{4,3,2,1,0:T(8,128)(2,1)S(1)}, u32[]{:S(2)}, u32[]{:S(2)}) collective-permute-start(bf16[2,2,14,8,128]{4,3,2,1,0:T(8,128)(2,1)S(1)} %slice.9), channel_id=1, source_target_pairs={{48,0},{0,16},{16,32},{32,48},{49,1},{1,17},{17,33},{33,49},{50,2}... | collective-permute-start | bytes 344072 | tf_op jit(solution)/shard_map/ppermute | solution.py:264
  29.6 8.1 %collective-permute-start.2 = (bf16[2,2,14,8,128]{4,3,2,1,0:T(8,128)(2,1)S(1)}, bf16[2,2,14,8,128]{4,3,2,1,0:T(8,128)(2,1)S(1)}, u32[]{:S(2)}, u32[]{:S(2)}) collective-permute-start(bf16[2,2,14,8,128]{4,3,2,1,0:T(8,128)(2,1)S(1)} %slice.8), channel_id=1, source_target_pairs={{16,0},{32,16},{48,32},{0,48},{17,1},{33,17},{49,33},{1,49},{18,2}... | collective-permute-start | bytes 344072 | tf_op jit(solution)/shard_map/ppermute | solution.py:264
  32.3 6.7 %collective-permute-start.5 = (bf16[4,2,14,8,128]{4,3,2,1,0:T(8,128)(2,1)S(1)}, bf16[4,2,14,8,128]{4,3,2,1,0:T(8,128)(2,1)S(1)}, u32[]{:S(2)}, u32[]{:S(2)}) collective-permute-start(bf16[4,2,14,8,128]{4,3,2,1,0:T(8,128)(2,1)S(1)} %collective-permute-done.refs_1_), channel_id=1, source_target_pairs={{0,4},{4,0},{1,5},{5,1},{2,6},{6,2},{3,7},{7,3},{8,12},{12,8},{9,1... | collective-permute-start | bytes 688136 | tf_op jit(solution)/shard_map/ppermute | solution.py:275
  32.3 6.7 %collective-permute-start.6 = (bf16[4,2,14,8,128]{4,3,2,1,0:T(8,128)(2,1)S(1)}, bf16[4,2,14,8,128]{4,3,2,1,0:T(8,128)(2,1)S(1)}, u32[]{:S(2)}, u32[]{:S(2)}) collective-permute-start(bf16[4,2,14,8,128]{4,3,2,1,0:T(8,128)(2,1)S(1)} %collective-permute-done.1.refs_2_), channel_id=1, source_target_pairs={{0,4},{4,0},{1,5},{5,1},{2,6},{6,2},{3,7},{7,3},{8,12},{12,8},{9,1... | collective-permute-start | bytes 688136 | tf_op jit(solution)/shard_map/ppermute | solution.py:275
  34.6 3.1 %collective-permute-start.8 = (bf16[2,2,14,8,128]{4,3,2,1,0:T(8,128)(2,1)S(1)}, bf16[2,2,14,8,128]{4,3,2,1,0:T(8,128)(2,1)S(1)}, u32[]{:S(2)}, u32[]{:S(2)}) collective-permute-start(bf16[2,2,14,8,128]{4,3,2,1,0:T(8,128)(2,1)S(1)} %collective-permute-done.3.refs_4_), channel_id=1, source_target_pairs={{0,4},{4,0},{1,5},{5,1},{2,6},{6,2},{3,7},{7,3},{8,12},{12,8},{9,1... | collective-permute-start | bytes 344072 | tf_op jit(solution)/shard_map/ppermute | solution.py:275
  37.7 1.3 %collective-permute-start.7 = (bf16[2,2,14,8,128]{4,3,2,1,0:T(8,128)(2,1)S(1)}, bf16[2,2,14,8,128]{4,3,2,1,0:T(8,128)(2,1)S(1)}, u32[]{:S(2)}, u32[]{:S(2)}) collective-permute-start(bf16[2,2,14,8,128]{4,3,2,1,0:T(8,128)(2,1)S(1)} %collective-permute-done.2.refs_3_), channel_id=1, source_target_pairs={{0,4},{4,0},{1,5},{5,1},{2,6},{6,2},{3,7},{7,3},{8,12},{12,8},{9,1... | collective-permute-start | bytes 344072 | tf_op jit(solution)/shard_map/ppermute | solution.py:275
  42.1 32.1 %copy-start = (bf16[4,13,128,128]{3,2,1,0:T(8,128)(2,1)S(1)}, bf16[4,13,128,128]{3,2,1,0:T(8,128)(2,1)}, u32[]{:S(2)}) copy-start(bf16[4,13,128,128]{3,2,1,0:T(8,128)(2,1)} %own.1) | copy-start | bytes 5111812
  77.0 5.0 %collective-permute-start.9 = (bf16[13,32,128]{2,1,0:T(8,128)(2,1)S(1)}, bf16[13,32,128]{2,1,0:T(8,128)(2,1)S(1)}, u32[]{:S(2)}, u32[]{:S(2)}) collective-permute-start(bf16[13,32,128]{2,1,0:T(8,128)(2,1)S(1)} %get-tuple-element.14), channel_id=1, source_target_pairs={{0,1},{1,2},{2,3},{3,0},{4,5},{5,6},{6,7},{7,4},{8,9},{9,10},{10,1... | collective-permute-start | bytes 319496 | tf_op jit(solution)/shard_map/ppermute | solution.py:280
  77.9 6.4 %collective-permute-start.10 = (bf16[13,32,128]{2,1,0:T(8,128)(2,1)S(1)}, bf16[13,32,128]{2,1,0:T(8,128)(2,1)S(1)}, u32[]{:S(2)}, u32[]{:S(2)}) collective-permute-start(bf16[13,32,128]{2,1,0:T(8,128)(2,1)S(1)} %get-tuple-element.15), channel_id=1, source_target_pairs={{0,2},{1,3},{2,0},{3,1},{4,6},{5,7},{6,4},{7,5},{8,10},{9,11},{10,... | collective-permute-start | bytes 319496 | tf_op jit(solution)/shard_map/ppermute | solution.py:280
  79.4 5.8 %collective-permute-start.11 = (bf16[13,32,128]{2,1,0:T(8,128)(2,1)S(1)}, bf16[13,32,128]{2,1,0:T(8,128)(2,1)S(1)}, u32[]{:S(2)}, u32[]{:S(2)}) collective-permute-start(bf16[13,32,128]{2,1,0:T(8,128)(2,1)S(1)} %get-tuple-element.16), channel_id=1, source_target_pairs={{0,3},{1,0},{2,1},{3,2},{4,7},{5,4},{6,5},{7,6},{8,11},{9,8},{10,9... | collective-permute-start | bytes 319496 | tf_op jit(solution)/shard_map/ppermute | solution.py:280
